TPU v7x, 32 devices: a whole 2x2x4 slice. The times are simulated.
32 devices in a mesh: tm: 4 (over z), feat: 8 (over y, x, core).
Axes of the slice: x: 2, y: 2, z: 4, core: 2. Of those that a mesh axis runs over, the one named last changes fastest.
Arguments:
- trajectory: float32 [16384, 2048], P('tm', 'feat'), may hold values from -8 to 9
Outputs:
- moments: float32 [4, 2048, 2048], P(None, 'feat', 'tm')
All inputs are finite; a program needn't handle non-finite values.
Results may differ from a plain program's by a relative error of at most 0.00035.
Values may be sent and summed in bfloat16 or wider, within the bound.
No kernel may reach another device: no remote copies, remote signals or barrier semaphores. Data moves between devices by JAX's collectives and lax.ppermute only.
A program may use at most 128 MiB of HBM per device.

v0:
```python
import math

import jax
import jax.numpy as jnp
from jax import lax
from jax.experimental import pallas as pl
from jax.experimental.pallas import tpu as pltpu
from jax.sharding import PartitionSpec as P


LAGS = (0, 1, 4, 16)
HALO = max(LAGS)


def bits(mask):
    return [b for b in range(mask.bit_length()) if mask >> b & 1]


def last_hop(mask, half):
    return bits(mask)[-1] if half == 0 else bits(mask)[0]


def arrivals(chips):
    singles = [m for m in range(1, chips) if len(bits(m)) == 1]
    order = [(m, i % 2) for i, m in enumerate(singles)]
    order += [(m, 1 - i % 2) for i, m in enumerate(singles)]
    if len(singles) % 2:
        order = [(m, h) for m in singles for h in (0, 1)]
    several = [m for m in range(1, chips) if len(bits(m)) > 1]
    order += [(m, h) for m in sorted(several, key=lambda m: len(bits(m))) for h in (0, 1)]
    return [order[i : i + 2] for i in range(0, len(order), 2)]


def tree_levels(q, count):
    def rep(low, size):
        if low <= q < low + size:
            return q
        return low + size - 1 if low + size <= q else low

    levels, size = [], 2
    while size <= count:
        moves = []
        for low in range(0, count, size):
            target = rep(low, size)
            a, b = rep(low, size // 2), rep(low + size // 2, size // 2)
            moves.append((a if target == b else b, target))
        levels.append(moves)
        size *= 2
    return levels


def chain_levels(q, count):
    return [
        [(k, k + 1)] * (k < q) + [(count - 1 - k, count - 2 - k)] * (count - 1 - k > q)
        for k in range(count - 1)
    ]


def lagged_kernel(*refs):
    out_ref, wide_ref, exact_ref = refs[-3:]
    rows, cols = wide_ref.shape[0] - HALO, wide_ref.shape[1]
    half = cols // 2
    step = pl.program_id(0)
    here = pl.ds(pl.multiple_of(step * rows, rows), rows)
    for i in (0, 1):
        first_ref, *parts = refs[5 * i : 5 * i + 5]
        for h in (0, 1):
            main_ref, prior_ref = parts[2 * h : 2 * h + 2]
            columns = slice(h * half, (h + 1) * half)
            prior = jnp.where(step == 0, first_ref[:, columns], prior_ref[...])
            exact_ref[:HALO, columns] = prior
            exact_ref[HALO:, columns] = main_ref[...]
            wide_ref[:HALO, columns] = prior.astype(jnp.float32)
            wide_ref[HALO:, columns] = main_ref[...].astype(jnp.float32)
        for k, lag in enumerate(LAGS):
            start = HALO - lag
            source = exact_ref if start % 16 == 0 else wide_ref
            at = (len(LAGS) * i + k) * cols
            out_ref[here, at : at + cols] = source[start : start + rows].astype(out_ref.dtype)


def lagged_columns(own, other):
    rows, half = own[1].shape
    cols = 2 * half
    step = math.gcd(rows, 512)
    wide = 2 * len(LAGS) * cols
    first = pl.BlockSpec((HALO, cols), lambda i: (0, 0))
    main = pl.BlockSpec((step, half), lambda i: (i, 0))
    prior = pl.BlockSpec((HALO, half), lambda i: (jnp.maximum(i * (step // HALO) - 1, 0), 0))
    operands = [v for before, a, b in (own, other) for v in (before, a, a, b, b)]
    return pl.pallas_call(
        lagged_kernel,
        out_shape=pltpu.VMEM((rows, wide), own[1].dtype),
        grid=(rows // step,),
        in_specs=[first, main, prior, main, prior] * 2,
        out_specs=pl.BlockSpec(memory_space=pltpu.VMEM),
        scratch_shapes=[
            pltpu.VMEM((step + HALO, cols), jnp.float32),
            pltpu.VMEM((step + HALO, cols), own[1].dtype),
        ],
        cost_estimate=pl.CostEstimate(
            flops=rows * wide, bytes_accessed=2 * rows * (wide + 2 * cols), transcendentals=0
        ),
        compiler_params=pltpu.CompilerParams(vmem_limit_bytes=16 * 1024 * 1024),
        name="lagged",
    )(*operands)


def join_kernel(left_ref, right_ref, out_ref, sems):
    cols = left_ref.shape[1]
    copies = [
        pltpu.make_async_copy(ref, out_ref.at[:, i * cols : (i + 1) * cols], sems.at[i])
        for i, ref in enumerate((left_ref, right_ref))
    ]
    for copy in copies:
        copy.start()
    for copy in copies:
        copy.wait()


def joined(left, right):
    rows, cols = left.shape
    anywhere = pl.BlockSpec(memory_space=pl.ANY)
    if cols % 128:
        return jnp.concatenate([left, right], 1)
    return pl.pallas_call(
        join_kernel,
        out_shape=pltpu.VMEM((rows, 2 * cols), left.dtype),
        in_specs=[anywhere, anywhere],
        out_specs=pl.BlockSpec(memory_space=pltpu.VMEM),
        scratch_shapes=[pltpu.SemaphoreType.DMA((2,))],
        cost_estimate=pl.CostEstimate(flops=0, bytes_accessed=8 * rows * cols, transcendentals=0),
        compiler_params=pltpu.CompilerParams(vmem_limit_bytes=1024 * 1024),
        name="join",
    )(left, right)


def order_kernel(flag_ref, a_ref, b_ref, lead_ref, rest_ref, sems):
    def copied(lead, rest):
        copies = [
            pltpu.make_async_copy(lead, lead_ref, sems.at[0]),
            pltpu.make_async_copy(rest, rest_ref, sems.at[1]),
        ]
        for copy in copies:
            copy.start()
        for copy in copies:
            copy.wait()

    @pl.when(flag_ref[0] == 1)
    def _():
        copied(a_ref, b_ref)

    @pl.when(flag_ref[0] != 1)
    def _():
        copied(b_ref, a_ref)


def ordered(flag, a, b):
    anywhere = pl.BlockSpec(memory_space=pl.ANY)
    return pl.pallas_call(
        order_kernel,
        out_shape=[pltpu.VMEM(a.shape, a.dtype)] * 2,
        in_specs=[pl.BlockSpec(memory_space=pltpu.SMEM), anywhere, anywhere],
        out_specs=[pl.BlockSpec(memory_space=pltpu.VMEM)] * 2,
        scratch_shapes=[pltpu.SemaphoreType.DMA((2,))],
        cost_estimate=pl.CostEstimate(
            flops=0, bytes_accessed=8 * a.shape[0] * a.shape[1], transcendentals=0
        ),
        compiler_params=pltpu.CompilerParams(vmem_limit_bytes=1024 * 1024),
        name="order",
    )(flag.astype(jnp.int32)[None], a, b)


def finish_kernel(core_ref, rows_ref, across_ref, *refs):
    out_ref = refs[-1]
    half = refs[0].shape[0]
    for i in (0, 1):
        owner = core_ref[0] if i == 0 else 1 - core_ref[0]
        for h in (0, 1):
            at = pl.ds(pl.multiple_of((2 * owner + h) * half, half), half)
            tall = rows_ref.shape[2]
            here = pl.ds(pl.multiple_of(pl.program_id(0) * tall, tall), tall)
            value = (refs[2 * i + h][:, here] * rows_ref[0]).T
            out_ref[0, :, at] = value * across_ref[:, at]


def finished(core, rows, across, pieces):
    lags, _, tall = rows.shape
    half = pieces[0].shape[0]
    wide = 4 * half
    if half % 128:
        order = lambda i: [jnp.where(core == i, pieces[h], pieces[2 + h]) for h in (0, 1)]
        value = jnp.concatenate(order(0) + order(1)).T.reshape(lags, tall, wide)
        return value * rows.transpose(0, 2, 1) * across
    return pl.pallas_call(
        finish_kernel,
        out_shape=jax.ShapeDtypeStruct((lags, tall, wide), jnp.float32),
        grid=(lags,),
        in_specs=[
            pl.BlockSpec(memory_space=pltpu.SMEM),
            pl.BlockSpec((1, 1, tall), lambda k: (k, 0, 0)),
            pl.BlockSpec((1, wide), lambda k: (0, 0)),
        ]
        + [pl.BlockSpec(memory_space=pltpu.VMEM)] * 4,
        out_specs=pl.BlockSpec((1, tall, wide), lambda k: (k, 0, 0)),
        cost_estimate=pl.CostEstimate(
            flops=2 * lags * tall * wide, bytes_accessed=8 * lags * tall * wide, transcendentals=0
        ),
        compiler_params=pltpu.CompilerParams(vmem_limit_bytes=16 * 1024 * 1024),
        name="finish",
    )(core[None], rows, across, *pieces)


def make(mesh):
    nz, nf = mesh.shape["tm"], mesh.shape["feat"]
    chips = nf // 2
    levels = nz.bit_length() - 1

    def shards(trajectory):
        rows, cols = trajectory.shape
        half = cols // 2
        tall = len(LAGS) * cols
        frames = rows * nz
        z, f = lax.axis_index("tm"), lax.axis_index("feat")
        chip, core = lax.div(f, 2), lax.rem(f, 2)
        mine = lax.bitwise_xor(chip, z)
        room = 2.0 ** math.floor(math.log2(32768.0 / frames))

        def hop(mask):
            return [(i, i ^ mask) for i in range(nf)]

        stats = jnp.stack([jnp.sum(trajectory, 0), jnp.max(trajectory, 0), jnp.min(trajectory, 0)])
        others = [
            lax.ppermute(stats, "tm", [(i, i ^ k) for i in range(nz)])
            for k in reversed(range(1, nz))
        ]
        total, high, low = stats
        for other in others:
            total = total + other[0]
            high, low = jnp.maximum(high, other[1]), jnp.minimum(low, other[2])
        mean = total / frames
        spread = high - low + jnp.maximum(jnp.abs(high), jnp.abs(low)) * 2.0**-14
        power = jnp.ceil(jnp.log2(jnp.maximum(spread, 2.0**-60)))
        shrink = lax.reduce_precision(jnp.exp2(-power), 8, 7)
        grow = lax.reduce_precision(jnp.exp2(power), 8, 7)

        def centre(value, low=0, high=cols):
            return ((value - mean[low:high]) * shrink[low:high]).astype(jnp.bfloat16)

        got = {}
        for h in (0, 1):
            low, high = h * half, (h + 1) * half
            got[0, h] = centre(trajectory[:, low:high], low, high)
            mean, shrink, got[0, h] = lax.optimization_barrier((mean, shrink, got[0, h]))
        slots = arrivals(chips)
        for slot in slots:
            for m, h in slot:
                if len(bits(m)) == 1:
                    got[m, h] = lax.ppermute(got[0, h], "feat", hop(2 * m))

        swapped = [lax.ppermute(got[0, h], "feat", hop(1)) for h in (0, 1)]
        tail, got[0, 1] = lax.optimization_barrier((trajectory, got[0, 1]))
        before = lax.ppermute(tail[rows - HALO :], "tm", [(i, i + 1) for i in range(nz - 1)])
        first = jnp.where(z == 0, jnp.bfloat16(0), centre(before))
        lagged = lagged_columns(
            (first, got[0, 0], got[0, 1]), (lax.ppermute(first, "feat", hop(1)), *swapped)
        )

        turned = lax.ppermute(grow[None], "feat", hop(1))[0]
        pair = jnp.stack([jnp.where(core == 0, grow, turned), jnp.where(core == 0, turned, grow)])
        across = pair
        for m in range(1, chips):
            across = jnp.where(mine == m, lax.ppermute(pair, "feat", hop(2 * m)), across)

        def product(block, low=0, high=2 * tall):
            value = lax.dot_general(
                block,
                lagged[:, low:high],
                (((0,), (0,)), ((), ())),
                preferred_element_type=jnp.float32,
            )
            return (value * room).astype(jnp.float16)

        def wide(value):
            return value.astype(jnp.float32)

        def rise(mask, level, flip=0, plan=tree_levels):
            return [
                (x * nf + j, y * nf + (j ^ flip))
                for j in range(nf)
                for x, y in plan(j // 2 ^ mask, nz)[level]
            ]

        both = ("tm", "feat")
        top = levels - 1
        none = jnp.float32(0)

        def add(values):
            total = wide(values[0])
            for value in values[1:]:
                total = total + wide(value)
            return total

        def climbed(part, mask, until, plan=tree_levels):
            terms = [part]
            for level in range(until):
                sent = part if level == 0 else add(terms).astype(jnp.float16)
                terms.append(lax.ppermute(sent, both, rise(mask, level, 0, plan)))
            return terms

        part = product(joined(got[0, 0], got[0, 1]))
        terms = climbed(part, 0, top)
        terms.append(lax.ppermute(add(terms).astype(jnp.float16), both, rise(0, top)))
        kept = [[(0, [v[h * half : (h + 1) * half] for v in terms])] for h in (0, 1)]

        for slot in slots:
            for m, h in slot:
                if len(bits(m)) > 1:
                    axis = 1 << last_hop(m, h)
                    got[m, h] = lax.ppermute(got[m ^ axis, h], "feat", hop(2 * axis))

        late = [[[], []], [[], []]]
        for slot in slots:
            (a, ha), (b, hb) = slot
            if a != b:
                low = (a ^ b) & -(a ^ b)
                flag = lax.bitwise_and(lax.bitwise_xor(mine, a), low) != 0
                blocks = ordered(flag, got[a, ha], got[b, hb])
                back = {}
                for leading, block in ((True, blocks[0]), (False, blocks[1])):
                    part = product(block)
                    for k in range(1, nz):
                        if bool(k & low) == leading:
                            pairs = [
                                (y * nf + i, (y ^ k) * nf + i)
                                for i in range(nf)
                                for y in range(nz)
                                if i // 2 ^ y ^ k in (a, b)
                            ]
                            back[k] = lax.ppermute(part, both, pairs)
                terms = [part] + [back[k] for k in sorted(back)]
                kept[ha].append((a, terms))
                kept[hb].append((b, terms))
                continue
            for h, plan in ((ha, chain_levels), (hb, tree_levels)):
                top = len(plan(0, nz)) - 1
                sides = []
                for i in (0, 1):
                    part = product(got[a, h], i * tall, (i + 1) * tall)
                    terms = climbed(part, a, top, plan)
                    sent = add(terms).astype(jnp.float16)
                    late[i][h].append(lax.ppermute(sent, both, rise(a, top, i, plan)))
                    sides.append(terms)
                kept[h].append((a, sides))

        def owned(m):
            terms = [dict(kept[h])[m] for h in (0, 1)]

            def branch():
                pieces = []
                for i in (0, 1):
                    for values in terms:
                        if isinstance(values[0], list):
                            values = values[i]
                        else:
                            values = [v[:, i * tall : (i + 1) * tall] for v in values]
                        pieces.append(add(values))
                return pieces

            return branch

        pieces = lax.switch(mine, [owned(m) for m in range(chips)])
        pieces = pieces[:2] + [lax.ppermute(pieces[2 + h], "feat", hop(1)) for h in (0, 1)]
        pieces = [add([v] + late[j // 2][j % 2]) for j, v in enumerate(pieces)]
        scales = 1 / (jnp.sqrt(jnp.float32(frames) - jnp.array(LAGS, jnp.float32)) * room)
        return finished(core, scales[:, None, None] * grow, across.reshape(1, 2 * cols), pieces)

    return shards


def plain(trajectory):
    rows = trajectory.shape[0]
    frames = rows * lax.axis_size("tm")
    mean = lax.psum(jnp.sum(trajectory, axis=0), "tm") / frames
    centered = (trajectory - mean).astype(jnp.bfloat16)
    gathered = lax.all_gather(centered, "feat", axis=1, tiled=True)
    steps = [(i, i - 1) for i in range(1, lax.axis_size("tm"))]
    tail = lax.ppermute(gathered[:HALO], "tm", steps)
    extended = jnp.concatenate([gathered, tail], axis=0)
    blocks = [
        lax.dot_general(
            centered,
            extended[lag : lag + rows],
            (((0,), (0,)), ((), ())),
            preferred_element_type=jnp.float32,
        )
        for lag in LAGS
    ]
    summed = lax.psum_scatter(jnp.stack(blocks), "tm", scatter_dimension=2, tiled=True)
    scales = jnp.sqrt(jnp.float32(frames) - jnp.array(LAGS, jnp.float32))
    return summed / scales[:, None, None]


def solution(mesh):
    nz, nf = mesh.shape["tm"], mesh.shape["feat"]
    paired = nf == 2 * nz and nz & (nz - 1) == 0 and nz > 2
    body = make(mesh) if paired else plain

    return jax.shard_map(
        body,
        mesh=mesh,
        in_specs=(P("tm", "feat"),),
        out_specs=P(None, "feat", "tm"),
        check_vma=False,
    )
```

profile of v0, /device:TPU:19, one launch (start us, length us, event | category | flops | bytes accessed | tf_op | source)
XLA Modules:
  0.0 202.1 jit_solution(17251235074163609834)
XLA Ops:
  0.0 2.9 %fusion.40 = (f32[256]{0:T(256)S(1)}, f32[256]{0:T(256)S(1)}, f32[256]{0:T(256)S(1)}) fusion(f32[4096,256]{1,0:T(8,128)} %param.6), kind=kLoop, calls=%fused_computation.70 | loop fusion | flops 3144960 | bytes 4197376 | tf_op jit(solution)/shard_map/reduce_sum | solution.py:232
  3.2 3.2 %collective-permute-start.1 = (f32[3,256]{1,0:T(4,128)S(1)}, f32[3,256]{1,0:T(4,128)S(1)}, u32[]{:S(2)}, u32[]{:S(2)}) collective-permute-start(f32[3,256]{1,0:T(4,128)S(1)} %pad_maximum_fusion), channel_id=1, source_target_pairs={{0,16},{8,24},{16,0},{24,8},{1,17},{9,25},{17,1},{25,9},{2,18},{10... | collective-permute-start | bytes 9224 | tf_op jit(solution)/shard_map/ppermute | solution.py:234
  7.4 1.4 collective-permute-done.2
  8.9 1.8 multiply_convert_fusion.1.left_ref.refs_1_.refs_2_
  11.0 1.3 collective-permute-start.14
  12.6 2.9 %collective-permute-start.3 = (f32[1,256]{1,0:T(1,128)S(1)}, f32[1,256]{1,0:T(1,128)S(1)}, u32[]{:S(2)}, u32[]{:S(2)}) collective-permute-start(f32[1,256]{1,0:T(1,128)S(1)} %get-tuple-element.159), channel_id=1, source_target_pairs={{0,1},{1,0},{2,3},{3,2},{4,5},{5,4},{6,7},{7,6},{8,9},{9,8},{10,11... | collective-permute-start | bytes 3080 | tf_op jit(solution)/shard_map/ppermute | solution.py:269
  17.6 16.5 %collective-permute-done.4 = f32[2,256]{1,0:T(2,128)S(1)} collective-permute-done((f32[2,256]{1,0:T(2,128)S(1)}, f32[2,256]{1,0:T(2,128)S(1)}, u32[]{:S(2)}, u32[]{:S(2)}) %collective-permute-start.4) | collective-permute-done | bytes 2080 | tf_op jit(solution)/shard_map/ppermute | solution.py:273
  36.9 2.8 %collective-permute-start.7 = (f32[16,256]{1,0:T(8,128)S(1)}, f32[16,256]{1,0:T(8,128)S(1)}, u32[]{:S(2)}, u32[]{:S(2)}) collective-permute-start(f32[16,256]{1,0:T(8,128)S(1)} %slice.227), channel_id=1, source_target_pairs={{0,8},{8,16},{16,24},{1,9},{9,17},{17,25},{2,10},{10,18},{18,26},{... | collective-permute-start | bytes 49160 | tf_op jit(solution)/shard_map/ppermute | solution.py:263
  41.6 2.2 %collective-permute-done.6 = f32[2,256]{1,0:T(2,128)S(1)} collective-permute-done((f32[2,256]{1,0:T(2,128)S(1)}, f32[2,256]{1,0:T(2,128)S(1)}, u32[]{:S(2)}, u32[]{:S(2)}) %collective-permute-start.6) | collective-permute-done | bytes 2080 | tf_op jit(solution)/shard_map/ppermute | solution.py:273
  45.0 7.7 %collective-permute-start.8 = (bf16[16,256]{1,0:T(8,128)(2,1)S(1)}, bf16[16,256]{1,0:T(8,128)(2,1)S(1)}, u32[]{:S(2)}, u32[]{:S(2)}) collective-permute-start(bf16[16,256]{1,0:T(8,128)(2,1)S(1)} %fusion.39.refs_0_), channel_id=1, source_target_pairs={{0,1},{1,0},{2,3},{3,2},{4,5},{5,4},{6,7},{7,6},{8,9},{9,8},{10,11... | collective-permute-start | bytes 24584 | tf_op jit(solution)/shard_map/ppermute | solution.py:266
  52.8 1.6 order.2
  54.4 6.3 %lagged.1 = bf16[4096,2048]{1,0:T(8,128)(2,1)S(1)} custom-call(bf16[16,256]{1,0:T(8,128)(2,1)S(1)} %fusion.39.refs_0_, bf16[4096,128]{1,0:T(8,128)(2,1)S(1)} %multiply_convert_fusion.1.left_ref.refs_1_.refs_2_, bf16[4096,128]{1,0:T(8,128)(2,1)S(1)} %multiply_convert_fusion.1.left_ref.refs_1_.refs_2_, ...), custom_call_target="tpu_custom_call" | custom-call | flops 8388608 | bytes 20971520 | tf_op jit(solution)/shard_map/lagged/pallas_call | solution.py:91
  60.7 2.4 %fusion.10 = f16[128,2048]{1,0:T(8,128)(2,1)S(1)} fusion(bf16[4096,128]{1,0:T(8,128)(2,1)S(1)} %get-tuple-element.126, bf16[4096,2048]{1,0:T(8,128)(2,1)S(1)} %lagged.1), kind=kOutput, calls=%fused_computation.31 | convolution fusion | flops 2148007936 | bytes 18350080 | tf_op jit(solution)/shard_map/dot_general | solution.py:276
  63.1 2.2 %collective-permute-start.15 = (f16[128,2048]{1,0:T(8,128)(2,1)S(1)}, f16[128,2048]{1,0:T(8,128)(2,1)S(1)}, u32[]{:S(2)}, u32[]{:S(2)}) collective-permute-start(f16[128,2048]{1,0:T(8,128)(2,1)S(1)} %fusion.10), channel_id=1, source_target_pairs={{0,8},{24,16},{1,9},{25,17},{10,2},{18,26},{11,3},{19,27},{12,4},{... | collective-permute-start | bytes 1572872 | tf_op jit(solution)/shard_map/ppermute | solution.py:340
  66.2 2.4 %fusion.12 = f16[128,2048]{1,0:T(8,128)(2,1)S(1)} fusion(bf16[4096,128]{1,0:T(8,128)(2,1)S(1)} %get-tuple-element.128, bf16[4096,2048]{1,0:T(8,128)(2,1)S(1)} %lagged.1), kind=kOutput, calls=%fused_computation.33 | convolution fusion | flops 2148007936 | bytes 18350080 | tf_op jit(solution)/shard_map/dot_general | solution.py:276
  68.6 2.5 %collective-permute-start.20 = (f16[128,2048]{1,0:T(8,128)(2,1)S(1)}, f16[128,2048]{1,0:T(8,128)(2,1)S(1)}, u32[]{:S(2)}, u32[]{:S(2)}) collective-permute-start(f16[128,2048]{1,0:T(8,128)(2,1)S(1)} %fusion.12), channel_id=1, source_target_pairs={{0,8},{24,16},{1,9},{25,17},{10,2},{18,26},{11,3},{19,27},{12,4},{... | collective-permute-start | bytes 1572872 | tf_op jit(solution)/shard_map/ppermute | solution.py:340
  71.8 2.4 %fusion.9 = f16[128,2048]{1,0:T(8,128)(2,1)S(1)} fusion(bf16[4096,128]{1,0:T(8,128)(2,1)S(1)} %get-tuple-element.125, bf16[4096,2048]{1,0:T(8,128)(2,1)S(1)} %lagged.1), kind=kOutput, calls=%fused_computation.30 | convolution fusion | flops 2148007936 | bytes 18350080 | tf_op jit(solution)/shard_map/dot_general | solution.py:276
  74.2 4.8 %collective-permute-start.16 = (f16[128,2048]{1,0:T(8,128)(2,1)S(1)}, f16[128,2048]{1,0:T(8,128)(2,1)S(1)}, u32[]{:S(2)}, u32[]{:S(2)}) collective-permute-start(f16[128,2048]{1,0:T(8,128)(2,1)S(1)} %fusion.9), channel_id=1, source_target_pairs={{0,16},{24,8},{1,17},{25,9},{10,26},{18,2},{11,27},{19,3},{12,28},... | collective-permute-start | bytes 1572872 | tf_op jit(solution)/shard_map/ppermute | solution.py:340
  79.0 2.4 %fusion.11 = f16[128,2048]{1,0:T(8,128)(2,1)S(1)} fusion(bf16[4096,128]{1,0:T(8,128)(2,1)S(1)} %get-tuple-element.127, bf16[4096,2048]{1,0:T(8,128)(2,1)S(1)} %lagged.1), kind=kOutput, calls=%fused_computation.32 | convolution fusion | flops 2148007936 | bytes 18350080 | tf_op jit(solution)/shard_map/dot_general | solution.py:276
  81.3 28.9 %collective-permute-done.15 = f16[128,2048]{1,0:T(8,128)(2,1)S(1)} collective-permute-done((f16[128,2048]{1,0:T(8,128)(2,1)S(1)}, f16[128,2048]{1,0:T(8,128)(2,1)S(1)}, u32[]{:S(2)}, u32[]{:S(2)}) %collective-permute-start.15) | collective-permute-done | bytes 524320 | tf_op jit(solution)/shard_map/ppermute | solution.py:340
  110.3 2.6 %collective-permute-start.21 = (f16[128,2048]{1,0:T(8,128)(2,1)S(1)}, f16[128,2048]{1,0:T(8,128)(2,1)S(1)}, u32[]{:S(2)}, u32[]{:S(2)}) collective-permute-start(f16[128,2048]{1,0:T(8,128)(2,1)S(1)} %fusion.11), channel_id=1, source_target_pairs={{0,16},{24,8},{1,17},{25,9},{10,26},{18,2},{11,27},{19,3},{12,28},... | collective-permute-start | bytes 1572872 | tf_op jit(solution)/shard_map/ppermute | solution.py:340
  113.0 1.4 collective-permute-start.23
  114.4 4.5 %fusion.8 = f16[256,2048]{1,0:T(8,128)(2,1)S(1)} fusion(bf16[4096,256]{1,0:T(8,128)(2,1)S(1)} %join.1, bf16[4096,2048]{1,0:T(8,128)(2,1)S(1)} %lagged.1), kind=kOutput, calls=%fused_computation.25 | convolution fusion | flops 4296015872 | bytes 19922944 | tf_op jit(solution)/shard_map/dot_general | solution.py:276
  118.9 13.8 %collective-permute-done.20 = f16[128,2048]{1,0:T(8,128)(2,1)S(1)} collective-permute-done((f16[128,2048]{1,0:T(8,128)(2,1)S(1)}, f16[128,2048]{1,0:T(8,128)(2,1)S(1)}, u32[]{:S(2)}, u32[]{:S(2)}) %collective-permute-start.20) | collective-permute-done | bytes 524320 | tf_op jit(solution)/shard_map/ppermute | solution.py:340
  132.7 1.3 collective-permute-start.11
  134.0 2.7 %collective-permute-done.26 = bf16[4096,128]{1,0:T(8,128)(2,1)S(1)} collective-permute-done((bf16[4096,128]{1,0:T(8,128)(2,1)}, bf16[4096,128]{1,0:T(8,128)(2,1)S(1)}, u32[]{:S(2)}, u32[]{:S(2)}) %collective-permute-start.26) | collective-permute-done | bytes 1048608 | tf_op jit(solution)/shard_map/ppermute | solution.py:320
  136.7 1.3 fusion.25
  138.0 1.3 collective-permute-start.30
  139.3 1.3 fusion.28
  140.6 1.3 collective-permute-start.28
  141.9 1.3 fusion.34
  143.2 1.3 collective-permute-start.24
  144.5 1.3 fusion.31
  145.8 1.3 collective-permute-start.27
  147.1 11.6 %collective-permute-done.11 = f16[256,2048]{1,0:T(8,128)(2,1)S(1)} collective-permute-done((f16[256,2048]{1,0:T(8,128)(2,1)S(1)}, f16[256,2048]{1,0:T(8,128)(2,1)S(1)}, u32[]{:S(2)}, u32[]{:S(2)}) %collective-permute-start.11) | collective-permute-done | bytes 1048608 | tf_op jit(solution)/shard_map/ppermute | solution.py:308
  159.1 1.6 collective-permute-start.12
  160.7 3.6 %collective-permute-done.30 = f16[128,1024]{1,0:T(8,128)(2,1)S(1)} collective-permute-done((f16[128,1024]{1,0:T(8,128)(2,1)S(1)}, f16[128,1024]{1,0:T(8,128)(2,1)S(1)}, u32[]{:S(2)}, u32[]{:S(2)}) %collective-permute-start.30) | collective-permute-done | bytes 262176 | tf_op jit(solution)/shard_map/ppermute | solution.py:308
  165.1 1.3 collective-permute-start.36
  166.4 9.1 %collective-permute-done.24 = f16[128,1024]{1,0:T(8,128)(2,1)S(1)} collective-permute-done((f16[128,1024]{1,0:T(8,128)(2,1)S(1)}, f16[128,1024]{1,0:T(8,128)(2,1)S(1)}, u32[]{:S(2)}, u32[]{:S(2)}) %collective-permute-start.24) | collective-permute-done | bytes 262176 | tf_op jit(solution)/shard_map/ppermute | solution.py:308
  175.6 1.3 collective-permute-start.25
  177.0 1.3 collective-permute-start.29
  178.3 2.8 %collective-permute-done.27 = f16[128,1024]{1,0:T(8,128)(2,1)S(1)} collective-permute-done((f16[128,1024]{1,0:T(8,128)(2,1)S(1)}, f16[128,1024]{1,0:T(8,128)(2,1)S(1)}, u32[]{:S(2)}, u32[]{:S(2)}) %collective-permute-start.27) | collective-permute-done | bytes 262176 | tf_op jit(solution)/shard_map/ppermute | solution.py:308
  182.0 1.3 collective-permute-start.32
  184.1 1.4 collective-permute-start.31
  185.5 2.7 %collective-permute-done.29 = f16[128,1024]{1,0:T(8,128)(2,1)S(1)} collective-permute-done((f16[128,1024]{1,0:T(8,128)(2,1)S(1)}, f16[128,1024]{1,0:T(8,128)(2,1)S(1)}, u32[]{:S(2)}, u32[]{:S(2)}) %collective-permute-start.29) | collective-permute-done | bytes 262176 | tf_op jit(solution)/shard_map/ppermute | solution.py:308
  188.7 6.5 %collective-permute-start.35 = (f32[128,1024]{1,0:T(8,128)S(1)}, f32[128,1024]{1,0:T(8,128)S(1)}, u32[]{:S(2)}, u32[]{:S(2)}) collective-permute-start(f32[128,1024]{1,0:T(8,128)S(1)} %get-tuple-element.132), channel_id=1, source_target_pairs={{0,1},{1,0},{2,3},{3,2},{4,5},{5,4},{6,7},{7,6},{8,9},{9,8},{10,11... | collective-permute-start | bytes 1572872 | tf_op jit(solution)/shard_map/ppermute | solution.py:373
  196.1 1.5 collective-permute-start.33
  199.9 2.2 %finish.1 = f32[4,256,512]{2,1,0:T(8,128)} custom-call(s32[1]{0:T(128)} %bitcast.core_ref, f32[4,1,256]{2,1,0:T(1,128)S(1)} %broadcast_multiply_fusion.rows_ref, f32[1,512]{1,0:T(1,128)S(1)} %bitcast.32, f32[128,1024]{1,0:T(8,128)S(1)} %convert_add_fusion.19.refs_0_, f32[128,1024]{1,0:T(8,128)S(1)} %convert_add_fusion.18.refs_1_, ...), custom_call_target="tpu_custom_call" | custom-call | flops 1048576 | bytes 4194304 | tf_op jit(solution)/shard_map/finish/pallas_call | solution.py:195
  (76 shorter events, 18.6 us)
Async XLA Ops:
  0.0 39.7 %copy-start.1 = (f32[4]{0:T(128)S(1)}, f32[4]{0:T(128)}, u32[]{:S(2)}) copy-start(f32[4]{0:T(128)} %constant.54) | copy-start | bytes 52
  0.0 10.8 %copy-start = (f32[4096,256]{1,0:T(8,128)S(1)}, f32[4096,256]{1,0:T(8,128)}, u32[]{:S(2)}) copy-start(f32[4096,256]{1,0:T(8,128)} %param.6) | copy-start | bytes 12582916
  2.9 3.4 %collective-permute-start = (f32[3,256]{1,0:T(4,128)S(1)}, f32[3,256]{1,0:T(4,128)S(1)}, u32[]{:S(2)}, u32[]{:S(2)}) collective-permute-start(f32[3,256]{1,0:T(4,128)S(1)} %pad_maximum_fusion), channel_id=1, source_target_pairs={{0,24},{8,16},{16,8},{24,0},{1,25},{9,17},{17,9},{25,1},{2,26},{10... | collective-permute-start | bytes 9224 | tf_op jit(solution)/shard_map/ppermute | solution.py:234
  3.2 4.2 %collective-permute-start.1 = (f32[3,256]{1,0:T(4,128)S(1)}, f32[3,256]{1,0:T(4,128)S(1)}, u32[]{:S(2)}, u32[]{:S(2)}) collective-permute-start(f32[3,256]{1,0:T(4,128)S(1)} %pad_maximum_fusion), channel_id=1, source_target_pairs={{0,16},{8,24},{16,0},{24,8},{1,17},{9,25},{17,1},{25,9},{2,18},{10... | collective-permute-start | bytes 9224 | tf_op jit(solution)/shard_map/ppermute | solution.py:234
  6.4 2.5 %collective-permute-start.2 = (f32[3,256]{1,0:T(4,128)S(1)}, f32[3,256]{1,0:T(4,128)S(1)}, u32[]{:S(2)}, u32[]{:S(2)}) collective-permute-start(f32[3,256]{1,0:T(4,128)S(1)} %pad_maximum_fusion), channel_id=1, source_target_pairs={{0,8},{8,0},{16,24},{24,16},{1,9},{9,1},{17,25},{25,17},{2,10},{10... | collective-permute-start | bytes 9224 | tf_op jit(solution)/shard_map/ppermute | solution.py:234
  11.0 33.1 %collective-permute-start.14 = (bf16[4096,128]{1,0:T(8,128)(2,1)S(1)}, bf16[4096,128]{1,0:T(8,128)(2,1)}, u32[]{:S(2)}, u32[]{:S(2)}) collective-permute-start(bf16[4096,128]{1,0:T(8,128)(2,1)S(1)} %multiply_convert_fusion.right_ref.refs_3_.refs_4_), channel_id=1, source_target_pairs={{0,4},{1,5},{2,6},{3,7},{4,0},{5,1},{6,2},{7,3},{8,12},{9,13},{10,... | collective-permute-start | bytes 3145736 | tf_op jit(solution)/shard_map/ppermute | solution.py:259
  12.3 32.7 %collective-permute-start.13 = (bf16[4096,128]{1,0:T(8,128)(2,1)S(1)}, bf16[4096,128]{1,0:T(8,128)(2,1)}, u32[]{:S(2)}, u32[]{:S(2)}) collective-permute-start(bf16[4096,128]{1,0:T(8,128)(2,1)S(1)} %multiply_convert_fusion.1.left_ref.refs_1_.refs_2_), channel_id=1, source_target_pairs={{0,2},{1,3},{2,0},{3,1},{4,6},{5,7},{6,4},{7,5},{8,10},{9,11},{10,... | collective-permute-start | bytes 3145736 | tf_op jit(solution)/shard_map/ppermute | solution.py:259
  12.6 3.8 %collective-permute-start.3 = (f32[1,256]{1,0:T(1,128)S(1)}, f32[1,256]{1,0:T(1,128)S(1)}, u32[]{:S(2)}, u32[]{:S(2)}) collective-permute-start(f32[1,256]{1,0:T(1,128)S(1)} %get-tuple-element.159), channel_id=1, source_target_pairs={{0,1},{1,0},{2,3},{3,2},{4,5},{5,4},{6,7},{7,6},{8,9},{9,8},{10,11... | collective-permute-start | bytes 3080 | tf_op jit(solution)/shard_map/ppermute | solution.py:269
  15.5 38.9 %collective-permute-start.10 = (bf16[4096,128]{1,0:T(8,128)(2,1)S(1)}, bf16[4096,128]{1,0:T(8,128)(2,1)S(1)}, u32[]{:S(2)}, u32[]{:S(2)}) collective-permute-start(bf16[4096,128]{1,0:T(8,128)(2,1)S(1)} %multiply_convert_fusion.right_ref.refs_3_.refs_4_), channel_id=1, source_target_pairs={{0,1},{1,0},{2,3},{3,2},{4,5},{5,4},{6,7},{7,6},{8,9},{9,8},{10,11... | collective-permute-start | bytes 3145736 | tf_op jit(solution)/shard_map/ppermute | solution.py:261
  15.5 38.9 %collective-permute-start.9 = (bf16[4096,128]{1,0:T(8,128)(2,1)S(1)}, bf16[4096,128]{1,0:T(8,128)(2,1)}, u32[]{:S(2)}, u32[]{:S(2)}) collective-permute-start(bf16[4096,128]{1,0:T(8,128)(2,1)S(1)} %multiply_convert_fusion.1.left_ref.refs_1_.refs_2_), channel_id=1, source_target_pairs={{0,1},{1,0},{2,3},{3,2},{4,5},{5,4},{6,7},{7,6},{8,9},{9,8},{10,11... | collective-permute-start | bytes 3145736 | tf_op jit(solution)/shard_map/ppermute | solution.py:261
  16.3 17.7 %collective-permute-start.4 = (f32[2,256]{1,0:T(2,128)S(1)}, f32[2,256]{1,0:T(2,128)S(1)}, u32[]{:S(2)}, u32[]{:S(2)}) collective-permute-start(f32[2,256]{1,0:T(2,128)S(1)} %pad_maximum_fusion.1), channel_id=1, source_target_pairs={{0,6},{1,7},{2,4},{3,5},{4,2},{5,3},{6,0},{7,1},{8,14},{9,15},{10,... | collective-permute-start | bytes 6152 | tf_op jit(solution)/shard_map/ppermute | solution.py:273
  34.1 2.8 %collective-permute-start.5 = (f32[2,256]{1,0:T(2,128)S(1)}, f32[2,256]{1,0:T(2,128)S(1)}, u32[]{:S(2)}, u32[]{:S(2)}) collective-permute-start(f32[2,256]{1,0:T(2,128)S(1)} %pad_maximum_fusion.1), channel_id=1, source_target_pairs={{0,4},{1,5},{2,6},{3,7},{4,0},{5,1},{6,2},{7,3},{8,12},{9,13},{10,... | collective-permute-start | bytes 6152 | tf_op jit(solution)/shard_map/ppermute | solution.py:273
  36.9 4.5 %collective-permute-start.7 = (f32[16,256]{1,0:T(8,128)S(1)}, f32[16,256]{1,0:T(8,128)S(1)}, u32[]{:S(2)}, u32[]{:S(2)}) collective-permute-start(f32[16,256]{1,0:T(8,128)S(1)} %slice.227), channel_id=1, source_target_pairs={{0,8},{8,16},{16,24},{1,9},{9,17},{17,25},{2,10},{10,18},{18,26},{... | collective-permute-start | bytes 49160 | tf_op jit(solution)/shard_map/ppermute | solution.py:263
  41.4 2.4 %collective-permute-start.6 = (f32[2,256]{1,0:T(2,128)S(1)}, f32[2,256]{1,0:T(2,128)S(1)}, u32[]{:S(2)}, u32[]{:S(2)}) collective-permute-start(f32[2,256]{1,0:T(2,128)S(1)} %pad_maximum_fusion.1), channel_id=1, source_target_pairs={{0,2},{1,3},{2,0},{3,1},{4,6},{5,7},{6,4},{7,5},{8,10},{9,11},{10,... | collective-permute-start | bytes 6152 | tf_op jit(solution)/shard_map/ppermute | solution.py:273
  43.8 22.2 %collective-permute-start.18 = (bf16[4096,128]{1,0:T(8,128)(2,1)S(1)}, bf16[4096,128]{1,0:T(8,128)(2,1)S(1)}, u32[]{:S(2)}, u32[]{:S(2)}) collective-permute-start(bf16[4096,128]{1,0:T(8,128)(2,1)S(1)} %multiply_convert_fusion.right_ref.refs_3_.refs_4_), channel_id=1, source_target_pairs={{0,2},{1,3},{2,0},{3,1},{4,6},{5,7},{6,4},{7,5},{8,10},{9,11},{10,... | collective-permute-start | bytes 3145736 | tf_op jit(solution)/shard_map/ppermute | solution.py:259
  44.1 22.0 %collective-permute-start.19 = (bf16[4096,128]{1,0:T(8,128)(2,1)S(1)}, bf16[4096,128]{1,0:T(8,128)(2,1)S(1)}, u32[]{:S(2)}, u32[]{:S(2)}) collective-permute-start(bf16[4096,128]{1,0:T(8,128)(2,1)S(1)} %multiply_convert_fusion.1.left_ref.refs_1_.refs_2_), channel_id=1, source_target_pairs={{0,4},{1,5},{2,6},{3,7},{4,0},{5,1},{6,2},{7,3},{8,12},{9,13},{10,... | collective-permute-start | bytes 3145736 | tf_op jit(solution)/shard_map/ppermute | solution.py:259
  45.0 9.3 %collective-permute-start.8 = (bf16[16,256]{1,0:T(8,128)(2,1)S(1)}, bf16[16,256]{1,0:T(8,128)(2,1)S(1)}, u32[]{:S(2)}, u32[]{:S(2)}) collective-permute-start(bf16[16,256]{1,0:T(8,128)(2,1)S(1)} %fusion.39.refs_0_), channel_id=1, source_target_pairs={{0,1},{1,0},{2,3},{3,2},{4,5},{5,4},{6,7},{7,6},{8,9},{9,8},{10,11... | collective-permute-start | bytes 24584 | tf_op jit(solution)/shard_map/ppermute | solution.py:266
  63.1 47.2 %collective-permute-start.15 = (f16[128,2048]{1,0:T(8,128)(2,1)S(1)}, f16[128,2048]{1,0:T(8,128)(2,1)S(1)}, u32[]{:S(2)}, u32[]{:S(2)}) collective-permute-start(f16[128,2048]{1,0:T(8,128)(2,1)S(1)} %fusion.10), channel_id=1, source_target_pairs={{0,8},{24,16},{1,9},{25,17},{10,2},{18,26},{11,3},{19,27},{12,4},{... | collective-permute-start | bytes 1572872 | tf_op jit(solution)/shard_map/ppermute | solution.py:340
  65.3 47.6 %collective-permute-start.17 = (f16[128,2048]{1,0:T(8,128)(2,1)S(1)}, f16[128,2048]{1,0:T(8,128)(2,1)S(1)}, u32[]{:S(2)}, u32[]{:S(2)}) collective-permute-start(f16[128,2048]{1,0:T(8,128)(2,1)S(1)} %fusion.10), channel_id=1, source_target_pairs={{8,16},{16,8},{9,17},{17,9},{2,26},{26,2},{3,27},{27,3},{4,28},{28... | collective-permute-start | bytes 1572872 | tf_op jit(solution)/shard_map/ppermute | solution.py:340
  68.6 64.1 %collective-permute-start.20 = (f16[128,2048]{1,0:T(8,128)(2,1)S(1)}, f16[128,2048]{1,0:T(8,128)(2,1)S(1)}, u32[]{:S(2)}, u32[]{:S(2)}) collective-permute-start(f16[128,2048]{1,0:T(8,128)(2,1)S(1)} %fusion.12), channel_id=1, source_target_pairs={{0,8},{24,16},{1,9},{25,17},{10,2},{18,26},{11,3},{19,27},{12,4},{... | collective-permute-start | bytes 1572872 | tf_op jit(solution)/shard_map/ppermute | solution.py:340
  71.1 62.9 %collective-permute-start.22 = (f16[128,2048]{1,0:T(8,128)(2,1)S(1)}, f16[128,2048]{1,0:T(8,128)(2,1)S(1)}, u32[]{:S(2)}, u32[]{:S(2)}) collective-permute-start(f16[128,2048]{1,0:T(8,128)(2,1)S(1)} %fusion.12), channel_id=1, source_target_pairs={{8,16},{16,8},{9,17},{17,9},{2,26},{26,2},{3,27},{27,3},{4,28},{28... | collective-permute-start | bytes 1572872 | tf_op jit(solution)/shard_map/ppermute | solution.py:340
  74.2 38.7 %collective-permute-start.16 = (f16[128,2048]{1,0:T(8,128)(2,1)S(1)}, f16[128,2048]{1,0:T(8,128)(2,1)S(1)}, u32[]{:S(2)}, u32[]{:S(2)}) collective-permute-start(f16[128,2048]{1,0:T(8,128)(2,1)S(1)} %fusion.9), channel_id=1, source_target_pairs={{0,16},{24,8},{1,17},{25,9},{10,26},{18,2},{11,27},{19,3},{12,28},... | collective-permute-start | bytes 1572872 | tf_op jit(solution)/shard_map/ppermute | solution.py:340
  110.3 23.8 %collective-permute-start.21 = (f16[128,2048]{1,0:T(8,128)(2,1)S(1)}, f16[128,2048]{1,0:T(8,128)(2,1)S(1)}, u32[]{:S(2)}, u32[]{:S(2)}) collective-permute-start(f16[128,2048]{1,0:T(8,128)(2,1)S(1)} %fusion.11), channel_id=1, source_target_pairs={{0,16},{24,8},{1,17},{25,9},{10,26},{18,2},{11,27},{19,3},{12,28},... | collective-permute-start | bytes 1572872 | tf_op jit(solution)/shard_map/ppermute | solution.py:340
  112.9 23.8 %collective-permute-start.26 = (bf16[4096,128]{1,0:T(8,128)(2,1)}, bf16[4096,128]{1,0:T(8,128)(2,1)S(1)}, u32[]{:S(2)}, u32[]{:S(2)}) collective-permute-start(bf16[4096,128]{1,0:T(8,128)(2,1)} %collective-permute-done.14.b_ref), channel_id=1, source_target_pairs={{0,2},{1,3},{2,0},{3,1},{4,6},{5,7},{6,4},{7,5},{8,10},{9,11},{10,... | collective-permute-start | bytes 3145736 | tf_op jit(solution)/shard_map/ppermute | solution.py:320
  113.0 26.3 %collective-permute-start.23 = (bf16[4096,128]{1,0:T(8,128)(2,1)}, bf16[4096,128]{1,0:T(8,128)(2,1)S(1)}, u32[]{:S(2)}, u32[]{:S(2)}) collective-permute-start(bf16[4096,128]{1,0:T(8,128)(2,1)} %collective-permute-done.13.a_ref), channel_id=1, source_target_pairs={{0,4},{1,5},{2,6},{3,7},{4,0},{5,1},{6,2},{7,3},{8,12},{9,13},{10,... | collective-permute-start | bytes 3145736 | tf_op jit(solution)/shard_map/ppermute | solution.py:320
  132.7 26.0 %collective-permute-start.11 = (f16[256,2048]{1,0:T(8,128)(2,1)S(1)}, f16[256,2048]{1,0:T(8,128)(2,1)S(1)}, u32[]{:S(2)}, u32[]{:S(2)}) collective-permute-start(f16[256,2048]{1,0:T(8,128)(2,1)S(1)} %fusion.8), channel_id=1, source_target_pairs={{8,0},{24,16},{9,1},{25,17},{2,10},{26,18},{3,11},{27,19},{4,12},{... | collective-permute-start | bytes 3145736 | tf_op jit(solution)/shard_map/ppermute | solution.py:308
  138.0 26.3 %collective-permute-start.30 = (f16[128,1024]{1,0:T(8,128)(2,1)S(1)}, f16[128,1024]{1,0:T(8,128)(2,1)S(1)}, u32[]{:S(2)}, u32[]{:S(2)}) collective-permute-start(f16[128,1024]{1,0:T(8,128)(2,1)S(1)} %fusion.25), channel_id=1, source_target_pairs={{0,8},{16,24},{1,9},{17,25},{2,10},{26,18},{3,11},{27,19},{4,12},{... | collective-permute-start | bytes 786440 | tf_op jit(solution)/shard_map/ppermute | solution.py:308
  140.6 36.4 %collective-permute-start.28 = (f16[128,1024]{1,0:T(8,128)(2,1)S(1)}, f16[128,1024]{1,0:T(8,128)(2,1)S(1)}, u32[]{:S(2)}, u32[]{:S(2)}) collective-permute-start(f16[128,1024]{1,0:T(8,128)(2,1)S(1)} %fusion.28), channel_id=1, source_target_pairs={{0,8},{1,9},{2,10},{26,18},{3,11},{27,19},{4,12},{28,20},{5,13},{2... | collective-permute-start | bytes 786440 | tf_op jit(solution)/shard_map/ppermute | solution.py:308
  143.2 32.4 %collective-permute-start.24 = (f16[128,1024]{1,0:T(8,128)(2,1)S(1)}, f16[128,1024]{1,0:T(8,128)(2,1)S(1)}, u32[]{:S(2)}, u32[]{:S(2)}) collective-permute-start(f16[128,1024]{1,0:T(8,128)(2,1)S(1)} %fusion.34), channel_id=1, source_target_pairs={{0,8},{1,9},{2,10},{26,18},{3,11},{27,19},{4,12},{28,20},{5,13},{2... | collective-permute-start | bytes 786440 | tf_op jit(solution)/shard_map/ppermute | solution.py:308
  145.8 35.4 %collective-permute-start.27 = (f16[128,1024]{1,0:T(8,128)(2,1)S(1)}, f16[128,1024]{1,0:T(8,128)(2,1)S(1)}, u32[]{:S(2)}, u32[]{:S(2)}) collective-permute-start(f16[128,1024]{1,0:T(8,128)(2,1)S(1)} %fusion.31), channel_id=1, source_target_pairs={{0,8},{16,24},{1,9},{17,25},{2,10},{26,18},{3,11},{27,19},{4,12},{... | collective-permute-start | bytes 786440 | tf_op jit(solution)/shard_map/ppermute | solution.py:308
  159.1 29.1 %collective-permute-start.12 = (f16[256,2048]{1,0:T(8,128)(2,1)S(1)}, f16[256,2048]{1,0:T(8,128)(2,1)S(1)}, u32[]{:S(2)}, u32[]{:S(2)}) collective-permute-start(f16[256,2048]{1,0:T(8,128)(2,1)S(1)} %add_convert_fusion), channel_id=1, source_target_pairs={{16,0},{17,1},{18,10},{19,11},{12,20},{13,21},{14,30},{15,31}} | collective-permute-start | bytes 3145736 | tf_op jit(solution)/shard_map/ppermute | solution.py:313
  165.1 34.5 %collective-permute-start.36 = (f16[128,1024]{1,0:T(8,128)(2,1)}, f16[128,1024]{1,0:T(8,128)(2,1)S(1)}, u32[]{:S(2)}, u32[]{:S(2)}) collective-permute-start(f16[128,1024]{1,0:T(8,128)(2,1)} %add_convert_fusion.1), channel_id=1, source_target_pairs={{8,25},{9,24},{10,19},{11,18},{20,13},{21,12},{22,7},{23,6}} | collective-permute-start | bytes 786440 | tf_op jit(solution)/shard_map/ppermute | solution.py:352
  175.6 7.6 %collective-permute-start.25 = (f16[128,1024]{1,0:T(8,128)(2,1)S(1)}, f16[128,1024]{1,0:T(8,128)(2,1)S(1)}, u32[]{:S(2)}, u32[]{:S(2)}) collective-permute-start(f16[128,1024]{1,0:T(8,128)(2,1)S(1)} %fusion.37), channel_id=1, source_target_pairs={{8,16},{9,17},{10,18},{11,19},{20,12},{21,13},{22,14},{23,15}} | collective-permute-start | bytes 786440 | tf_op jit(solution)/shard_map/ppermute | solution.py:308
  177.0 11.2 %collective-permute-start.29 = (f16[128,1024]{1,0:T(8,128)(2,1)S(1)}, f16[128,1024]{1,0:T(8,128)(2,1)S(1)}, u32[]{:S(2)}, u32[]{:S(2)}) collective-permute-start(f16[128,1024]{1,0:T(8,128)(2,1)S(1)} %fusion.38), channel_id=1, source_target_pairs={{8,16},{9,17},{10,18},{11,19},{20,12},{21,13},{22,14},{23,15}} | collective-permute-start | bytes 786440 | tf_op jit(solution)/shard_map/ppermute | solution.py:308
  182.0 14.1 %collective-permute-start.32 = (f16[128,1024]{1,0:T(8,128)(2,1)}, f16[128,1024]{1,0:T(8,128)(2,1)}, u32[]{:S(2)}, u32[]{:S(2)}) collective-permute-start(f16[128,1024]{1,0:T(8,128)(2,1)} %add_convert_fusion.3), channel_id=1, source_target_pairs={{8,24},{9,25},{10,18},{11,19},{20,12},{21,13},{22,6},{23,7}} | collective-permute-start | bytes 786440 | tf_op jit(solution)/shard_map/ppermute | solution.py:352
  184.1 14.5 %collective-permute-start.31 = (f16[128,1024]{1,0:T(8,128)(2,1)}, f16[128,1024]{1,0:T(8,128)(2,1)}, u32[]{:S(2)}, u32[]{:S(2)}) collective-permute-start(f16[128,1024]{1,0:T(8,128)(2,1)} %add_convert_fusion.4), channel_id=1, source_target_pairs={{16,24},{17,25},{14,6},{15,7}} | collective-permute-start | bytes 786440 | tf_op jit(solution)/shard_map/ppermute | solution.py:352
  188.7 11.0 %collective-permute-start.35 = (f32[128,1024]{1,0:T(8,128)S(1)}, f32[128,1024]{1,0:T(8,128)S(1)}, u32[]{:S(2)}, u32[]{:S(2)}) collective-permute-start(f32[128,1024]{1,0:T(8,128)S(1)} %get-tuple-element.132), channel_id=1, source_target_pairs={{0,1},{1,0},{2,3},{3,2},{4,5},{5,4},{6,7},{7,6},{8,9},{9,8},{10,11... | collective-permute-start | bytes 1572872 | tf_op jit(solution)/shard_map/ppermute | solution.py:373
  195.4 4.4 %collective-permute-start.34 = (f16[128,1024]{1,0:T(8,128)(2,1)S(1)}, f16[128,1024]{1,0:T(8,128)(2,1)S(1)}, u32[]{:S(2)}, u32[]{:S(2)}) collective-permute-start(f16[128,1024]{1,0:T(8,128)(2,1)S(1)} %add_convert_fusion.2), channel_id=1, source_target_pairs={{16,25},{17,24},{14,7},{15,6}} | collective-permute-start | bytes 786440 | tf_op jit(solution)/shard_map/ppermute | solution.py:352
  196.1 3.7 %collective-permute-start.33 = (f32[128,1024]{1,0:T(8,128)S(1)}, f32[128,1024]{1,0:T(8,128)S(1)}, u32[]{:S(2)}, u32[]{:S(2)}) collective-permute-start(f32[128,1024]{1,0:T(8,128)S(1)} %get-tuple-element.131), channel_id=1, source_target_pairs={{0,1},{1,0},{2,3},{3,2},{4,5},{5,4},{6,7},{7,6},{8,9},{9,8},{10,11... | collective-permute-start | bytes 1572872 | tf_op jit(solution)/shard_map/ppermute | solution.py:373
where the time goes:
time: 203 us; the launch traced here: 202 us
  waiting for transfers between devices  98.9 us (49%)
  starting transfers between devices  61.1 us (30%)
  matrix products  19.1 us (9%)
  other arithmetic  11 us (5%)
  Pallas kernels  10.7 us (5%)
    ppermute x6, waiting for transfers between devices, shards(): back[k] = lax.ppermute(part, both, pairs)  42.7 us
    ppermute x7, waiting for transfers between devices, climbed(): terms.append(lax.ppermute(sent, both, rise(mask, level, 0, plan)))  29.9 us
    ppermute x3, waiting for transfers between devices, shards(): lax.ppermute(pair, 'feat', hop(2 * m))  19.5 us
    dot_general x9, matrix products, product(): lax.dot_general(block, lagged[:, low:high], (((0,), (0,)), ((), ())), pre...  19.1 us
    ppermute x6, starting transfers between devices, shards(): back[k] = lax.ppermute(part, both, pairs)  13.5 us
    ppermute x7, starting transfers between devices, climbed(): terms.append(lax.ppermute(sent, both, rise(mask, level, 0, plan)))  9.03 us
    ppermute x2, starting transfers between devices, shards(): lax.ppermute(pieces[2 + h], 'feat', hop(1))  8.04 us
    ppermute x1, starting transfers between devices, shards(): lax.ppermute(first, 'feat', hop(1))  7.73 us
  transfers between devices with their start and end apart: 37, of which 15 were waited for; matrix products, arithmetic and copies ran while one was open for 13% of the time, Pallas kernels for 4%

commit v1 on v0

--- a/solution.py
+++ b/solution.py
@@ -178,9 +178,7 @@
         owner = core_ref[0] if i == 0 else 1 - core_ref[0]
         for h in (0, 1):
             at = pl.ds(pl.multiple_of((2 * owner + h) * half, half), half)
-            tall = rows_ref.shape[2]
-            here = pl.ds(pl.multiple_of(pl.program_id(0) * tall, tall), tall)
-            value = (refs[2 * i + h][:, here] * rows_ref[0]).T
+            value = (refs[2 * i + h][...] * rows_ref[0]).T
             out_ref[0, :, at] = value * across_ref[:, at]
 
 
@@ -201,7 +199,7 @@
             pl.BlockSpec((1, 1, tall), lambda k: (k, 0, 0)),
             pl.BlockSpec((1, wide), lambda k: (0, 0)),
         ]
-        + [pl.BlockSpec(memory_space=pltpu.VMEM)] * 4,
+        + [pl.BlockSpec((half, tall), lambda k: (0, k))] * 4,
         out_specs=pl.BlockSpec((1, tall, wide), lambda k: (k, 0, 0)),
         cost_estimate=pl.CostEstimate(
             flops=2 * lags * tall * wide, bytes_accessed=8 * lags * tall * wide, transcendentals=0
@@ -342,10 +340,11 @@
                 kept[ha].append((a, terms))
                 kept[hb].append((b, terms))
                 continue
-            for h, plan in ((ha, chain_levels), (hb, tree_levels)):
-                top = len(plan(0, nz)) - 1
+            for h in (ha, hb):
                 sides = []
                 for i in (0, 1):
+                    plan = chain_levels if (h, i) == (ha, 0) else tree_levels
+                    top = len(plan(0, nz)) - 1
                     part = product(got[a, h], i * tall, (i + 1) * tall)
                     terms = climbed(part, a, top, plan)
                     sent = add(terms).astype(jnp.float16)

time: 203 us -> 200 us (0.985)
    ppermute x7 -> x6, waiting for transfers between devices: 29.9 us -> 24.9 us  [climbed(): terms.append(lax.ppermute(sent, both, rise(mask, level, 0, plan)))]
    ppermute x4, waiting for transfers between devices: 0.01 us -> 4.95 us  [shards(): late[i][h].append(lax.ppermute(sent, both, rise(a, top, i, plan)))]
    ppermute x7 -> x6, starting transfers between devices: 9.03 us -> 7.96 us  [climbed(): terms.append(lax.ppermute(sent, both, rise(mask, level, 0, plan)))]
  transfers between devices with their start and end apart: 37 -> 36, of which waited for: 15 -> 16; matrix products, arithmetic and copies ran while one was open for 13% -> 12% of each run, Pallas kernels for 4% -> 4%
where the time goes in v1:
time: 200 us
  waiting for transfers between devices  98.8 us (49%)
  starting transfers between devices  60.5 us (30%)
  matrix products  19.2 us (10%)
  Pallas kernels  10.9 us (5%)
  other arithmetic  9.17 us (5%)
    ppermute x6, waiting for transfers between devices, shards(): back[k] = lax.ppermute(part, both, pairs)  42.7 us
    ppermute x6, waiting for transfers between devices, climbed(): terms.append(lax.ppermute(sent, both, rise(mask, level, 0, plan)))  24.9 us
    ppermute x3, waiting for transfers between devices, shards(): lax.ppermute(pair, 'feat', hop(2 * m))  19.5 us
    dot_general x9, matrix products, product(): lax.dot_general(block, lagged[:, low:high], (((0,), (0,)), ((), ())), pre...  19.2 us
    ppermute x6, starting transfers between devices, shards(): back[k] = lax.ppermute(part, both, pairs)  13.5 us
    ppermute x2, starting transfers between devices, shards(): lax.ppermute(pieces[2 + h], 'feat', hop(1))  8.09 us
    ppermute x6, starting transfers between devices, climbed(): terms.append(lax.ppermute(sent, both, rise(mask, level, 0, plan)))  7.96 us
    ppermute x1, starting transfers between devices, shards(): lax.ppermute(first, 'feat', hop(1))  7.73 us
  transfers between devices with their start and end apart: 36, of which 16 were waited for; matrix products, arithmetic and copies ran while one was open for 12% of the time, Pallas kernels for 4%

profile of v1, /device:TPU:19, one launch (start us, length us, event | category | flops | bytes accessed | tf_op | source)
XLA Modules:
  0.0 199.8 jit_solution(8585450950582919249)
XLA Ops:
  0.0 2.9 %fusion.39 = (f32[256]{0:T(256)S(1)}, f32[256]{0:T(256)S(1)}, f32[256]{0:T(256)S(1)}) fusion(f32[4096,256]{1,0:T(8,128)} %param.6), kind=kLoop, calls=%fused_computation.68 | loop fusion | flops 3144960 | bytes 4197376 | tf_op jit(solution)/shard_map/reduce_sum | solution.py:230
  3.2 3.2 %collective-permute-start.1 = (f32[3,256]{1,0:T(4,128)S(1)}, f32[3,256]{1,0:T(4,128)S(1)}, u32[]{:S(2)}, u32[]{:S(2)}) collective-permute-start(f32[3,256]{1,0:T(4,128)S(1)} %pad_maximum_fusion), channel_id=1, source_target_pairs={{0,16},{8,24},{16,0},{24,8},{1,17},{9,25},{17,1},{25,9},{2,18},{10... | collective-permute-start | bytes 9224 | tf_op jit(solution)/shard_map/ppermute | solution.py:232
  7.4 1.4 collective-permute-done.2
  8.9 1.8 multiply_convert_fusion.1.left_ref.refs_1_.refs_2_
  11.0 1.3 collective-permute-start.14
  12.6 2.9 %collective-permute-start.3 = (f32[1,256]{1,0:T(1,128)S(1)}, f32[1,256]{1,0:T(1,128)S(1)}, u32[]{:S(2)}, u32[]{:S(2)}) collective-permute-start(f32[1,256]{1,0:T(1,128)S(1)} %get-tuple-element.156), channel_id=1, source_target_pairs={{0,1},{1,0},{2,3},{3,2},{4,5},{5,4},{6,7},{7,6},{8,9},{9,8},{10,11... | collective-permute-start | bytes 3080 | tf_op jit(solution)/shard_map/ppermute | solution.py:267
  17.6 16.5 %collective-permute-done.4 = f32[2,256]{1,0:T(2,128)S(1)} collective-permute-done((f32[2,256]{1,0:T(2,128)S(1)}, f32[2,256]{1,0:T(2,128)S(1)}, u32[]{:S(2)}, u32[]{:S(2)}) %collective-permute-start.4) | collective-permute-done | bytes 2080 | tf_op jit(solution)/shard_map/ppermute | solution.py:271
  36.9 2.8 %collective-permute-start.7 = (f32[16,256]{1,0:T(8,128)S(1)}, f32[16,256]{1,0:T(8,128)S(1)}, u32[]{:S(2)}, u32[]{:S(2)}) collective-permute-start(f32[16,256]{1,0:T(8,128)S(1)} %slice.227), channel_id=1, source_target_pairs={{0,8},{8,16},{16,24},{1,9},{9,17},{17,25},{2,10},{10,18},{18,26},{... | collective-permute-start | bytes 49160 | tf_op jit(solution)/shard_map/ppermute | solution.py:261
  41.6 2.2 %collective-permute-done.6 = f32[2,256]{1,0:T(2,128)S(1)} collective-permute-done((f32[2,256]{1,0:T(2,128)S(1)}, f32[2,256]{1,0:T(2,128)S(1)}, u32[]{:S(2)}, u32[]{:S(2)}) %collective-permute-start.6) | collective-permute-done | bytes 2080 | tf_op jit(solution)/shard_map/ppermute | solution.py:271
  45.0 7.7 %collective-permute-start.8 = (bf16[16,256]{1,0:T(8,128)(2,1)S(1)}, bf16[16,256]{1,0:T(8,128)(2,1)S(1)}, u32[]{:S(2)}, u32[]{:S(2)}) collective-permute-start(bf16[16,256]{1,0:T(8,128)(2,1)S(1)} %fusion.38.refs_0_), channel_id=1, source_target_pairs={{0,1},{1,0},{2,3},{3,2},{4,5},{5,4},{6,7},{7,6},{8,9},{9,8},{10,11... | collective-permute-start | bytes 24584 | tf_op jit(solution)/shard_map/ppermute | solution.py:264
  52.8 1.6 order.2
  54.4 6.3 %lagged.1 = bf16[4096,2048]{1,0:T(8,128)(2,1)S(1)} custom-call(bf16[16,256]{1,0:T(8,128)(2,1)S(1)} %fusion.38.refs_0_, bf16[4096,128]{1,0:T(8,128)(2,1)S(1)} %multiply_convert_fusion.1.left_ref.refs_1_.refs_2_, bf16[4096,128]{1,0:T(8,128)(2,1)S(1)} %multiply_convert_fusion.1.left_ref.refs_1_.refs_2_, ...), custom_call_target="tpu_custom_call" | custom-call | flops 8388608 | bytes 20971520 | tf_op jit(solution)/shard_map/lagged/pallas_call | solution.py:91
  60.7 2.4 %fusion.10 = f16[128,2048]{1,0:T(8,128)(2,1)S(1)} fusion(bf16[4096,128]{1,0:T(8,128)(2,1)S(1)} %get-tuple-element.123, bf16[4096,2048]{1,0:T(8,128)(2,1)S(1)} %lagged.1), kind=kOutput, calls=%fused_computation.31 | convolution fusion | flops 2148007936 | bytes 18350080 | tf_op jit(solution)/shard_map/dot_general | solution.py:274
  63.1 2.2 %collective-permute-start.15 = (f16[128,2048]{1,0:T(8,128)(2,1)S(1)}, f16[128,2048]{1,0:T(8,128)(2,1)S(1)}, u32[]{:S(2)}, u32[]{:S(2)}) collective-permute-start(f16[128,2048]{1,0:T(8,128)(2,1)S(1)} %fusion.10), channel_id=1, source_target_pairs={{0,8},{24,16},{1,9},{25,17},{10,2},{18,26},{11,3},{19,27},{12,4},{... | collective-permute-start | bytes 1572872 | tf_op jit(solution)/shard_map/ppermute | solution.py:338
  66.3 2.4 %fusion.12 = f16[128,2048]{1,0:T(8,128)(2,1)S(1)} fusion(bf16[4096,128]{1,0:T(8,128)(2,1)S(1)} %get-tuple-element.125, bf16[4096,2048]{1,0:T(8,128)(2,1)S(1)} %lagged.1), kind=kOutput, calls=%fused_computation.33 | convolution fusion | flops 2148007936 | bytes 18350080 | tf_op jit(solution)/shard_map/dot_general | solution.py:274
  68.7 2.5 %collective-permute-start.20 = (f16[128,2048]{1,0:T(8,128)(2,1)S(1)}, f16[128,2048]{1,0:T(8,128)(2,1)S(1)}, u32[]{:S(2)}, u32[]{:S(2)}) collective-permute-start(f16[128,2048]{1,0:T(8,128)(2,1)S(1)} %fusion.12), channel_id=1, source_target_pairs={{0,8},{24,16},{1,9},{25,17},{10,2},{18,26},{11,3},{19,27},{12,4},{... | collective-permute-start | bytes 1572872 | tf_op jit(solution)/shard_map/ppermute | solution.py:338
  71.9 2.4 %fusion.9 = f16[128,2048]{1,0:T(8,128)(2,1)S(1)} fusion(bf16[4096,128]{1,0:T(8,128)(2,1)S(1)} %get-tuple-element.122, bf16[4096,2048]{1,0:T(8,128)(2,1)S(1)} %lagged.1), kind=kOutput, calls=%fused_computation.30 | convolution fusion | flops 2148007936 | bytes 18350080 | tf_op jit(solution)/shard_map/dot_general | solution.py:274
  74.3 4.8 %collective-permute-start.16 = (f16[128,2048]{1,0:T(8,128)(2,1)S(1)}, f16[128,2048]{1,0:T(8,128)(2,1)S(1)}, u32[]{:S(2)}, u32[]{:S(2)}) collective-permute-start(f16[128,2048]{1,0:T(8,128)(2,1)S(1)} %fusion.9), channel_id=1, source_target_pairs={{0,16},{24,8},{1,17},{25,9},{10,26},{18,2},{11,27},{19,3},{12,28},... | collective-permute-start | bytes 1572872 | tf_op jit(solution)/shard_map/ppermute | solution.py:338
  79.0 2.4 %fusion.11 = f16[128,2048]{1,0:T(8,128)(2,1)S(1)} fusion(bf16[4096,128]{1,0:T(8,128)(2,1)S(1)} %get-tuple-element.124, bf16[4096,2048]{1,0:T(8,128)(2,1)S(1)} %lagged.1), kind=kOutput, calls=%fused_computation.32 | convolution fusion | flops 2148007936 | bytes 18350080 | tf_op jit(solution)/shard_map/dot_general | solution.py:274
  81.4 28.9 %collective-permute-done.15 = f16[128,2048]{1,0:T(8,128)(2,1)S(1)} collective-permute-done((f16[128,2048]{1,0:T(8,128)(2,1)S(1)}, f16[128,2048]{1,0:T(8,128)(2,1)S(1)}, u32[]{:S(2)}, u32[]{:S(2)}) %collective-permute-start.15) | collective-permute-done | bytes 524320 | tf_op jit(solution)/shard_map/ppermute | solution.py:338
  110.3 2.6 %collective-permute-start.21 = (f16[128,2048]{1,0:T(8,128)(2,1)S(1)}, f16[128,2048]{1,0:T(8,128)(2,1)S(1)}, u32[]{:S(2)}, u32[]{:S(2)}) collective-permute-start(f16[128,2048]{1,0:T(8,128)(2,1)S(1)} %fusion.11), channel_id=1, source_target_pairs={{0,16},{24,8},{1,17},{25,9},{10,26},{18,2},{11,27},{19,3},{12,28},... | collective-permute-start | bytes 1572872 | tf_op jit(solution)/shard_map/ppermute | solution.py:338
  113.0 1.4 collective-permute-start.23
  114.4 4.5 %fusion.8 = f16[256,2048]{1,0:T(8,128)(2,1)S(1)} fusion(bf16[4096,256]{1,0:T(8,128)(2,1)S(1)} %join.1, bf16[4096,2048]{1,0:T(8,128)(2,1)S(1)} %lagged.1), kind=kOutput, calls=%fused_computation.25 | convolution fusion | flops 4296015872 | bytes 19922944 | tf_op jit(solution)/shard_map/dot_general | solution.py:274
  119.0 13.8 %collective-permute-done.20 = f16[128,2048]{1,0:T(8,128)(2,1)S(1)} collective-permute-done((f16[128,2048]{1,0:T(8,128)(2,1)S(1)}, f16[128,2048]{1,0:T(8,128)(2,1)S(1)}, u32[]{:S(2)}, u32[]{:S(2)}) %collective-permute-start.20) | collective-permute-done | bytes 524320 | tf_op jit(solution)/shard_map/ppermute | solution.py:338
  132.8 1.3 collective-permute-start.11
  134.1 2.6 %collective-permute-done.26 = bf16[4096,128]{1,0:T(8,128)(2,1)S(1)} collective-permute-done((bf16[4096,128]{1,0:T(8,128)(2,1)}, bf16[4096,128]{1,0:T(8,128)(2,1)S(1)}, u32[]{:S(2)}, u32[]{:S(2)}) %collective-permute-start.26) | collective-permute-done | bytes 1048608 | tf_op jit(solution)/shard_map/ppermute | solution.py:318
  138.0 1.3 collective-permute-start.29
  139.3 1.3 fusion.34
  140.6 1.3 collective-permute-start.24
  141.9 1.3 fusion.31
  143.2 1.3 collective-permute-start.27
  144.5 14.2 %collective-permute-done.11 = f16[256,2048]{1,0:T(8,128)(2,1)S(1)} collective-permute-done((f16[256,2048]{1,0:T(8,128)(2,1)S(1)}, f16[256,2048]{1,0:T(8,128)(2,1)S(1)}, u32[]{:S(2)}, u32[]{:S(2)}) %collective-permute-start.11) | collective-permute-done | bytes 1048608 | tf_op jit(solution)/shard_map/ppermute | solution.py:306
  159.3 1.4 collective-permute-start.12
  160.6 1.3 fusion.28
  162.0 1.5 collective-permute-start.28
  163.5 6.5 %collective-permute-done.24 = f16[128,1024]{1,0:T(8,128)(2,1)S(1)} collective-permute-done((f16[128,1024]{1,0:T(8,128)(2,1)S(1)}, f16[128,1024]{1,0:T(8,128)(2,1)S(1)}, u32[]{:S(2)}, u32[]{:S(2)}) %collective-permute-start.24) | collective-permute-done | bytes 262176 | tf_op jit(solution)/shard_map/ppermute | solution.py:306
  170.1 1.3 collective-permute-start.25
  171.5 1.3 collective-permute-start.35
  172.8 2.8 %collective-permute-done.27 = f16[128,1024]{1,0:T(8,128)(2,1)S(1)} collective-permute-done((f16[128,1024]{1,0:T(8,128)(2,1)S(1)}, f16[128,1024]{1,0:T(8,128)(2,1)S(1)}, u32[]{:S(2)}, u32[]{:S(2)}) %collective-permute-start.27) | collective-permute-done | bytes 262176 | tf_op jit(solution)/shard_map/ppermute | solution.py:306
  176.4 1.3 collective-permute-start.31
  178.6 1.4 collective-permute-start.30
  179.9 1.3 collective-permute-done.28
  181.7 4.1 %collective-permute-start.34 = (f32[128,1024]{1,0:T(8,128)S(1)}, f32[128,1024]{1,0:T(8,128)S(1)}, u32[]{:S(2)}, u32[]{:S(2)}) collective-permute-start(f32[128,1024]{1,0:T(8,128)S(1)} %get-tuple-element.129), channel_id=1, source_target_pairs={{0,1},{1,0},{2,3},{3,2},{4,5},{5,4},{6,7},{7,6},{8,9},{9,8},{10,11... | collective-permute-start | bytes 1572872 | tf_op jit(solution)/shard_map/ppermute | solution.py:372
  185.9 1.3 collective-permute-start.33
  187.2 2.8 %collective-permute-done.31 = f16[128,1024]{1,0:T(8,128)(2,1)S(1)} collective-permute-done((f16[128,1024]{1,0:T(8,128)(2,1)}, f16[128,1024]{1,0:T(8,128)(2,1)S(1)}, u32[]{:S(2)}, u32[]{:S(2)}) %collective-permute-start.31) | collective-permute-done | bytes 262176 | tf_op jit(solution)/shard_map/ppermute | solution.py:351
  190.0 3.9 %collective-permute-start.32 = (f32[128,1024]{1,0:T(8,128)S(1)}, f32[128,1024]{1,0:T(8,128)S(1)}, u32[]{:S(2)}, u32[]{:S(2)}) collective-permute-start(f32[128,1024]{1,0:T(8,128)S(1)} %get-tuple-element.128), channel_id=1, source_target_pairs={{0,1},{1,0},{2,3},{3,2},{4,5},{5,4},{6,7},{7,6},{8,9},{9,8},{10,11... | collective-permute-start | bytes 1572872 | tf_op jit(solution)/shard_map/ppermute | solution.py:372
  195.2 2.1 %collective-permute-done.33 = f16[128,1024]{1,0:T(8,128)(2,1)S(1)} collective-permute-done((f16[128,1024]{1,0:T(8,128)(2,1)S(1)}, f16[128,1024]{1,0:T(8,128)(2,1)S(1)}, u32[]{:S(2)}, u32[]{:S(2)}) %collective-permute-start.33) | collective-permute-done | bytes 262176 | tf_op jit(solution)/shard_map/ppermute | solution.py:351
  197.4 2.4 %finish.1 = f32[4,256,512]{2,1,0:T(8,128)} custom-call(s32[1]{0:T(128)} %bitcast.core_ref, f32[4,1,256]{2,1,0:T(1,128)S(1)} %broadcast_multiply_fusion.rows_ref, f32[1,512]{1,0:T(1,128)S(1)} %bitcast.32, f32[128,1024]{1,0:T(8,128)S(1)} %convert_add_fusion.19.refs_0_, f32[128,1024]{1,0:T(8,128)S(1)} %convert_add_fusion.18.refs_1_, ...), custom_call_target="tpu_custom_call" | custom-call | flops 1048576 | bytes 4194304 | tf_op jit(solution)/shard_map/finish/pallas_call | solution.py:193
  (73 shorter events, 17.3 us)
Async XLA Ops:
  0.0 39.7 %copy-start.1 = (f32[4]{0:T(128)S(1)}, f32[4]{0:T(128)}, u32[]{:S(2)}) copy-start(f32[4]{0:T(128)} %constant.54) | copy-start | bytes 52
  0.0 10.8 %copy-start = (f32[4096,256]{1,0:T(8,128)S(1)}, f32[4096,256]{1,0:T(8,128)}, u32[]{:S(2)}) copy-start(f32[4096,256]{1,0:T(8,128)} %param.6) | copy-start | bytes 12582916
  2.9 3.4 %collective-permute-start = (f32[3,256]{1,0:T(4,128)S(1)}, f32[3,256]{1,0:T(4,128)S(1)}, u32[]{:S(2)}, u32[]{:S(2)}) collective-permute-start(f32[3,256]{1,0:T(4,128)S(1)} %pad_maximum_fusion), channel_id=1, source_target_pairs={{0,24},{8,16},{16,8},{24,0},{1,25},{9,17},{17,9},{25,1},{2,26},{10... | collective-permute-start | bytes 9224 | tf_op jit(solution)/shard_map/ppermute | solution.py:232
  3.2 4.2 %collective-permute-start.1 = (f32[3,256]{1,0:T(4,128)S(1)}, f32[3,256]{1,0:T(4,128)S(1)}, u32[]{:S(2)}, u32[]{:S(2)}) collective-permute-start(f32[3,256]{1,0:T(4,128)S(1)} %pad_maximum_fusion), channel_id=1, source_target_pairs={{0,16},{8,24},{16,0},{24,8},{1,17},{9,25},{17,1},{25,9},{2,18},{10... | collective-permute-start | bytes 9224 | tf_op jit(solution)/shard_map/ppermute | solution.py:232
  6.4 2.5 %collective-permute-start.2 = (f32[3,256]{1,0:T(4,128)S(1)}, f32[3,256]{1,0:T(4,128)S(1)}, u32[]{:S(2)}, u32[]{:S(2)}) collective-permute-start(f32[3,256]{1,0:T(4,128)S(1)} %pad_maximum_fusion), channel_id=1, source_target_pairs={{0,8},{8,0},{16,24},{24,16},{1,9},{9,1},{17,25},{25,17},{2,10},{10... | collective-permute-start | bytes 9224 | tf_op jit(solution)/shard_map/ppermute | solution.py:232
  11.0 33.1 %collective-permute-start.14 = (bf16[4096,128]{1,0:T(8,128)(2,1)S(1)}, bf16[4096,128]{1,0:T(8,128)(2,1)}, u32[]{:S(2)}, u32[]{:S(2)}) collective-permute-start(bf16[4096,128]{1,0:T(8,128)(2,1)S(1)} %multiply_convert_fusion.right_ref.refs_3_.refs_4_), channel_id=1, source_target_pairs={{0,4},{1,5},{2,6},{3,7},{4,0},{5,1},{6,2},{7,3},{8,12},{9,13},{10,... | collective-permute-start | bytes 3145736 | tf_op jit(solution)/shard_map/ppermute | solution.py:257
  12.3 32.7 %collective-permute-start.13 = (bf16[4096,128]{1,0:T(8,128)(2,1)S(1)}, bf16[4096,128]{1,0:T(8,128)(2,1)}, u32[]{:S(2)}, u32[]{:S(2)}) collective-permute-start(bf16[4096,128]{1,0:T(8,128)(2,1)S(1)} %multiply_convert_fusion.1.left_ref.refs_1_.refs_2_), channel_id=1, source_target_pairs={{0,2},{1,3},{2,0},{3,1},{4,6},{5,7},{6,4},{7,5},{8,10},{9,11},{10,... | collective-permute-start | bytes 3145736 | tf_op jit(solution)/shard_map/ppermute | solution.py:257
  12.6 3.8 %collective-permute-start.3 = (f32[1,256]{1,0:T(1,128)S(1)}, f32[1,256]{1,0:T(1,128)S(1)}, u32[]{:S(2)}, u32[]{:S(2)}) collective-permute-start(f32[1,256]{1,0:T(1,128)S(1)} %get-tuple-element.156), channel_id=1, source_target_pairs={{0,1},{1,0},{2,3},{3,2},{4,5},{5,4},{6,7},{7,6},{8,9},{9,8},{10,11... | collective-permute-start | bytes 3080 | tf_op jit(solution)/shard_map/ppermute | solution.py:267
  15.5 38.9 %collective-permute-start.10 = (bf16[4096,128]{1,0:T(8,128)(2,1)S(1)}, bf16[4096,128]{1,0:T(8,128)(2,1)S(1)}, u32[]{:S(2)}, u32[]{:S(2)}) collective-permute-start(bf16[4096,128]{1,0:T(8,128)(2,1)S(1)} %multiply_convert_fusion.right_ref.refs_3_.refs_4_), channel_id=1, source_target_pairs={{0,1},{1,0},{2,3},{3,2},{4,5},{5,4},{6,7},{7,6},{8,9},{9,8},{10,11... | collective-permute-start | bytes 3145736 | tf_op jit(solution)/shard_map/ppermute | solution.py:259
  15.5 38.9 %collective-permute-start.9 = (bf16[4096,128]{1,0:T(8,128)(2,1)S(1)}, bf16[4096,128]{1,0:T(8,128)(2,1)}, u32[]{:S(2)}, u32[]{:S(2)}) collective-permute-start(bf16[4096,128]{1,0:T(8,128)(2,1)S(1)} %multiply_convert_fusion.1.left_ref.refs_1_.refs_2_), channel_id=1, source_target_pairs={{0,1},{1,0},{2,3},{3,2},{4,5},{5,4},{6,7},{7,6},{8,9},{9,8},{10,11... | collective-permute-start | bytes 3145736 | tf_op jit(solution)/shard_map/ppermute | solution.py:259
  16.3 17.7 %collective-permute-start.4 = (f32[2,256]{1,0:T(2,128)S(1)}, f32[2,256]{1,0:T(2,128)S(1)}, u32[]{:S(2)}, u32[]{:S(2)}) collective-permute-start(f32[2,256]{1,0:T(2,128)S(1)} %pad_maximum_fusion.1), channel_id=1, source_target_pairs={{0,6},{1,7},{2,4},{3,5},{4,2},{5,3},{6,0},{7,1},{8,14},{9,15},{10,... | collective-permute-start | bytes 6152 | tf_op jit(solution)/shard_map/ppermute | solution.py:271
  34.1 2.8 %collective-permute-start.5 = (f32[2,256]{1,0:T(2,128)S(1)}, f32[2,256]{1,0:T(2,128)S(1)}, u32[]{:S(2)}, u32[]{:S(2)}) collective-permute-start(f32[2,256]{1,0:T(2,128)S(1)} %pad_maximum_fusion.1), channel_id=1, source_target_pairs={{0,4},{1,5},{2,6},{3,7},{4,0},{5,1},{6,2},{7,3},{8,12},{9,13},{10,... | collective-permute-start | bytes 6152 | tf_op jit(solution)/shard_map/ppermute | solution.py:271
  36.9 4.5 %collective-permute-start.7 = (f32[16,256]{1,0:T(8,128)S(1)}, f32[16,256]{1,0:T(8,128)S(1)}, u32[]{:S(2)}, u32[]{:S(2)}) collective-permute-start(f32[16,256]{1,0:T(8,128)S(1)} %slice.227), channel_id=1, source_target_pairs={{0,8},{8,16},{16,24},{1,9},{9,17},{17,25},{2,10},{10,18},{18,26},{... | collective-permute-start | bytes 49160 | tf_op jit(solution)/shard_map/ppermute | solution.py:261
  41.4 2.4 %collective-permute-start.6 = (f32[2,256]{1,0:T(2,128)S(1)}, f32[2,256]{1,0:T(2,128)S(1)}, u32[]{:S(2)}, u32[]{:S(2)}) collective-permute-start(f32[2,256]{1,0:T(2,128)S(1)} %pad_maximum_fusion.1), channel_id=1, source_target_pairs={{0,2},{1,3},{2,0},{3,1},{4,6},{5,7},{6,4},{7,5},{8,10},{9,11},{10,... | collective-permute-start | bytes 6152 | tf_op jit(solution)/shard_map/ppermute | solution.py:271
  43.8 22.3 %collective-permute-start.18 = (bf16[4096,128]{1,0:T(8,128)(2,1)S(1)}, bf16[4096,128]{1,0:T(8,128)(2,1)S(1)}, u32[]{:S(2)}, u32[]{:S(2)}) collective-permute-start(bf16[4096,128]{1,0:T(8,128)(2,1)S(1)} %multiply_convert_fusion.right_ref.refs_3_.refs_4_), channel_id=1, source_target_pairs={{0,2},{1,3},{2,0},{3,1},{4,6},{5,7},{6,4},{7,5},{8,10},{9,11},{10,... | collective-permute-start | bytes 3145736 | tf_op jit(solution)/shard_map/ppermute | solution.py:257
  44.1 22.0 %collective-permute-start.19 = (bf16[4096,128]{1,0:T(8,128)(2,1)S(1)}, bf16[4096,128]{1,0:T(8,128)(2,1)S(1)}, u32[]{:S(2)}, u32[]{:S(2)}) collective-permute-start(bf16[4096,128]{1,0:T(8,128)(2,1)S(1)} %multiply_convert_fusion.1.left_ref.refs_1_.refs_2_), channel_id=1, source_target_pairs={{0,4},{1,5},{2,6},{3,7},{4,0},{5,1},{6,2},{7,3},{8,12},{9,13},{10,... | collective-permute-start | bytes 3145736 | tf_op jit(solution)/shard_map/ppermute | solution.py:257
  45.0 9.3 %collective-permute-start.8 = (bf16[16,256]{1,0:T(8,128)(2,1)S(1)}, bf16[16,256]{1,0:T(8,128)(2,1)S(1)}, u32[]{:S(2)}, u32[]{:S(2)}) collective-permute-start(bf16[16,256]{1,0:T(8,128)(2,1)S(1)} %fusion.38.refs_0_), channel_id=1, source_target_pairs={{0,1},{1,0},{2,3},{3,2},{4,5},{5,4},{6,7},{7,6},{8,9},{9,8},{10,11... | collective-permute-start | bytes 24584 | tf_op jit(solution)/shard_map/ppermute | solution.py:264
  63.1 47.2 %collective-permute-start.15 = (f16[128,2048]{1,0:T(8,128)(2,1)S(1)}, f16[128,2048]{1,0:T(8,128)(2,1)S(1)}, u32[]{:S(2)}, u32[]{:S(2)}) collective-permute-start(f16[128,2048]{1,0:T(8,128)(2,1)S(1)} %fusion.10), channel_id=1, source_target_pairs={{0,8},{24,16},{1,9},{25,17},{10,2},{18,26},{11,3},{19,27},{12,4},{... | collective-permute-start | bytes 1572872 | tf_op jit(solution)/shard_map/ppermute | solution.py:338
  65.4 47.6 %collective-permute-start.17 = (f16[128,2048]{1,0:T(8,128)(2,1)S(1)}, f16[128,2048]{1,0:T(8,128)(2,1)S(1)}, u32[]{:S(2)}, u32[]{:S(2)}) collective-permute-start(f16[128,2048]{1,0:T(8,128)(2,1)S(1)} %fusion.10), channel_id=1, source_target_pairs={{8,16},{16,8},{9,17},{17,9},{2,26},{26,2},{3,27},{27,3},{4,28},{28... | collective-permute-start | bytes 1572872 | tf_op jit(solution)/shard_map/ppermute | solution.py:338
  68.7 64.1 %collective-permute-start.20 = (f16[128,2048]{1,0:T(8,128)(2,1)S(1)}, f16[128,2048]{1,0:T(8,128)(2,1)S(1)}, u32[]{:S(2)}, u32[]{:S(2)}) collective-permute-start(f16[128,2048]{1,0:T(8,128)(2,1)S(1)} %fusion.12), channel_id=1, source_target_pairs={{0,8},{24,16},{1,9},{25,17},{10,2},{18,26},{11,3},{19,27},{12,4},{... | collective-permute-start | bytes 1572872 | tf_op jit(solution)/shard_map/ppermute | solution.py:338
  71.2 62.9 %collective-permute-start.22 = (f16[128,2048]{1,0:T(8,128)(2,1)S(1)}, f16[128,2048]{1,0:T(8,128)(2,1)S(1)}, u32[]{:S(2)}, u32[]{:S(2)}) collective-permute-start(f16[128,2048]{1,0:T(8,128)(2,1)S(1)} %fusion.12), channel_id=1, source_target_pairs={{8,16},{16,8},{9,17},{17,9},{2,26},{26,2},{3,27},{27,3},{4,28},{28... | collective-permute-start | bytes 1572872 | tf_op jit(solution)/shard_map/ppermute | solution.py:338
  74.3 38.7 %collective-permute-start.16 = (f16[128,2048]{1,0:T(8,128)(2,1)S(1)}, f16[128,2048]{1,0:T(8,128)(2,1)S(1)}, u32[]{:S(2)}, u32[]{:S(2)}) collective-permute-start(f16[128,2048]{1,0:T(8,128)(2,1)S(1)} %fusion.9), channel_id=1, source_target_pairs={{0,16},{24,8},{1,17},{25,9},{10,26},{18,2},{11,27},{19,3},{12,28},... | collective-permute-start | bytes 1572872 | tf_op jit(solution)/shard_map/ppermute | solution.py:338
  110.3 23.8 %collective-permute-start.21 = (f16[128,2048]{1,0:T(8,128)(2,1)S(1)}, f16[128,2048]{1,0:T(8,128)(2,1)S(1)}, u32[]{:S(2)}, u32[]{:S(2)}) collective-permute-start(f16[128,2048]{1,0:T(8,128)(2,1)S(1)} %fusion.11), channel_id=1, source_target_pairs={{0,16},{24,8},{1,17},{25,9},{10,26},{18,2},{11,27},{19,3},{12,28},... | collective-permute-start | bytes 1572872 | tf_op jit(solution)/shard_map/ppermute | solution.py:338
  112.9 23.8 %collective-permute-start.26 = (bf16[4096,128]{1,0:T(8,128)(2,1)}, bf16[4096,128]{1,0:T(8,128)(2,1)S(1)}, u32[]{:S(2)}, u32[]{:S(2)}) collective-permute-start(bf16[4096,128]{1,0:T(8,128)(2,1)} %collective-permute-done.14.b_ref), channel_id=1, source_target_pairs={{0,2},{1,3},{2,0},{3,1},{4,6},{5,7},{6,4},{7,5},{8,10},{9,11},{10,... | collective-permute-start | bytes 3145736 | tf_op jit(solution)/shard_map/ppermute | solution.py:318
  113.0 26.3 %collective-permute-start.23 = (bf16[4096,128]{1,0:T(8,128)(2,1)}, bf16[4096,128]{1,0:T(8,128)(2,1)S(1)}, u32[]{:S(2)}, u32[]{:S(2)}) collective-permute-start(bf16[4096,128]{1,0:T(8,128)(2,1)} %collective-permute-done.13.a_ref), channel_id=1, source_target_pairs={{0,4},{1,5},{2,6},{3,7},{4,0},{5,1},{6,2},{7,3},{8,12},{9,13},{10,... | collective-permute-start | bytes 3145736 | tf_op jit(solution)/shard_map/ppermute | solution.py:318
  132.8 26.0 %collective-permute-start.11 = (f16[256,2048]{1,0:T(8,128)(2,1)S(1)}, f16[256,2048]{1,0:T(8,128)(2,1)S(1)}, u32[]{:S(2)}, u32[]{:S(2)}) collective-permute-start(f16[256,2048]{1,0:T(8,128)(2,1)S(1)} %fusion.8), channel_id=1, source_target_pairs={{8,0},{24,16},{9,1},{25,17},{2,10},{26,18},{3,11},{27,19},{4,12},{... | collective-permute-start | bytes 3145736 | tf_op jit(solution)/shard_map/ppermute | solution.py:306
  138.0 33.4 %collective-permute-start.29 = (f16[128,1024]{1,0:T(8,128)(2,1)S(1)}, f16[128,1024]{1,0:T(8,128)(2,1)S(1)}, u32[]{:S(2)}, u32[]{:S(2)}) collective-permute-start(f16[128,1024]{1,0:T(8,128)(2,1)S(1)} %fusion.25), channel_id=1, source_target_pairs={{0,8},{16,24},{1,9},{17,25},{2,10},{26,18},{3,11},{27,19},{4,12},{... | collective-permute-start | bytes 786440 | tf_op jit(solution)/shard_map/ppermute | solution.py:306
  140.6 29.4 %collective-permute-start.24 = (f16[128,1024]{1,0:T(8,128)(2,1)S(1)}, f16[128,1024]{1,0:T(8,128)(2,1)S(1)}, u32[]{:S(2)}, u32[]{:S(2)}) collective-permute-start(f16[128,1024]{1,0:T(8,128)(2,1)S(1)} %fusion.34), channel_id=1, source_target_pairs={{0,8},{1,9},{2,10},{26,18},{3,11},{27,19},{4,12},{28,20},{5,13},{2... | collective-permute-start | bytes 786440 | tf_op jit(solution)/shard_map/ppermute | solution.py:306
  143.2 32.4 %collective-permute-start.27 = (f16[128,1024]{1,0:T(8,128)(2,1)S(1)}, f16[128,1024]{1,0:T(8,128)(2,1)S(1)}, u32[]{:S(2)}, u32[]{:S(2)}) collective-permute-start(f16[128,1024]{1,0:T(8,128)(2,1)S(1)} %fusion.31), channel_id=1, source_target_pairs={{0,8},{16,24},{1,9},{17,25},{2,10},{26,18},{3,11},{27,19},{4,12},{... | collective-permute-start | bytes 786440 | tf_op jit(solution)/shard_map/ppermute | solution.py:306
  159.3 22.0 %collective-permute-start.12 = (f16[256,2048]{1,0:T(8,128)(2,1)S(1)}, f16[256,2048]{1,0:T(8,128)(2,1)S(1)}, u32[]{:S(2)}, u32[]{:S(2)}) collective-permute-start(f16[256,2048]{1,0:T(8,128)(2,1)S(1)} %add_convert_fusion), channel_id=1, source_target_pairs={{16,0},{17,1},{18,10},{19,11},{12,20},{13,21},{14,30},{15,31}} | collective-permute-start | bytes 3145736 | tf_op jit(solution)/shard_map/ppermute | solution.py:311
  162.0 19.3 %collective-permute-start.28 = (f16[128,1024]{1,0:T(8,128)(2,1)S(1)}, f16[128,1024]{1,0:T(8,128)(2,1)S(1)}, u32[]{:S(2)}, u32[]{:S(2)}) collective-permute-start(f16[128,1024]{1,0:T(8,128)(2,1)S(1)} %fusion.28), channel_id=1, source_target_pairs={{0,8},{16,24},{1,9},{17,25},{2,10},{26,18},{3,11},{27,19},{4,12},{... | collective-permute-start | bytes 786440 | tf_op jit(solution)/shard_map/ppermute | solution.py:306
  170.1 7.6 %collective-permute-start.25 = (f16[128,1024]{1,0:T(8,128)(2,1)S(1)}, f16[128,1024]{1,0:T(8,128)(2,1)S(1)}, u32[]{:S(2)}, u32[]{:S(2)}) collective-permute-start(f16[128,1024]{1,0:T(8,128)(2,1)S(1)} %fusion.37), channel_id=1, source_target_pairs={{8,16},{9,17},{10,18},{11,19},{20,12},{21,13},{22,14},{23,15}} | collective-permute-start | bytes 786440 | tf_op jit(solution)/shard_map/ppermute | solution.py:306
  171.5 23.6 %collective-permute-start.35 = (f16[128,1024]{1,0:T(8,128)(2,1)S(1)}, f16[128,1024]{1,0:T(8,128)(2,1)S(1)}, u32[]{:S(2)}, u32[]{:S(2)}) collective-permute-start(f16[128,1024]{1,0:T(8,128)(2,1)S(1)} %add_convert_fusion.1), channel_id=1, source_target_pairs={{8,25},{9,24},{10,19},{11,18},{20,13},{21,12},{22,7},{23,6}} | collective-permute-start | bytes 786440 | tf_op jit(solution)/shard_map/ppermute | solution.py:351
  176.4 13.6 %collective-permute-start.31 = (f16[128,1024]{1,0:T(8,128)(2,1)}, f16[128,1024]{1,0:T(8,128)(2,1)S(1)}, u32[]{:S(2)}, u32[]{:S(2)}) collective-permute-start(f16[128,1024]{1,0:T(8,128)(2,1)} %add_convert_fusion.3), channel_id=1, source_target_pairs={{8,24},{9,25},{10,18},{11,19},{20,12},{21,13},{22,6},{23,7}} | collective-permute-start | bytes 786440 | tf_op jit(solution)/shard_map/ppermute | solution.py:351
  178.6 15.5 %collective-permute-start.30 = (f16[128,1024]{1,0:T(8,128)(2,1)}, f16[128,1024]{1,0:T(8,128)(2,1)}, u32[]{:S(2)}, u32[]{:S(2)}) collective-permute-start(f16[128,1024]{1,0:T(8,128)(2,1)} %add_convert_fusion.4), channel_id=1, source_target_pairs={{16,24},{17,25},{14,6},{15,7}} | collective-permute-start | bytes 786440 | tf_op jit(solution)/shard_map/ppermute | solution.py:351
  181.7 13.4 %collective-permute-start.34 = (f32[128,1024]{1,0:T(8,128)S(1)}, f32[128,1024]{1,0:T(8,128)S(1)}, u32[]{:S(2)}, u32[]{:S(2)}) collective-permute-start(f32[128,1024]{1,0:T(8,128)S(1)} %get-tuple-element.129), channel_id=1, source_target_pairs={{0,1},{1,0},{2,3},{3,2},{4,5},{5,4},{6,7},{7,6},{8,9},{9,8},{10,11... | collective-permute-start | bytes 1572872 | tf_op jit(solution)/shard_map/ppermute | solution.py:372
  185.9 11.4 %collective-permute-start.33 = (f16[128,1024]{1,0:T(8,128)(2,1)S(1)}, f16[128,1024]{1,0:T(8,128)(2,1)S(1)}, u32[]{:S(2)}, u32[]{:S(2)}) collective-permute-start(f16[128,1024]{1,0:T(8,128)(2,1)S(1)} %add_convert_fusion.2), channel_id=1, source_target_pairs={{8,25},{9,24},{10,19},{11,18},{20,13},{21,12},{22,7},{23,6}} | collective-permute-start | bytes 786440 | tf_op jit(solution)/shard_map/ppermute | solution.py:351
  190.0 7.3 %collective-permute-start.32 = (f32[128,1024]{1,0:T(8,128)S(1)}, f32[128,1024]{1,0:T(8,128)S(1)}, u32[]{:S(2)}, u32[]{:S(2)}) collective-permute-start(f32[128,1024]{1,0:T(8,128)S(1)} %get-tuple-element.128), channel_id=1, source_target_pairs={{0,1},{1,0},{2,3},{3,2},{4,5},{5,4},{6,7},{7,6},{8,9},{9,8},{10,11... | collective-permute-start | bytes 1572872 | tf_op jit(solution)/shard_map/ppermute | solution.py:372
